TPU v7x, 32 devices: a whole 2x2x4 slice. The times are simulated.
32 devices in a mesh: blk: 8 (over z, x), tile: 4 (over y, core).
Axes of the slice: x: 2, y: 2, z: 4, core: 2. Of those that a mesh axis runs over, the one named last changes fastest.
Arguments:
- stream_in: bfloat16 [32, 16, 16, 2240], P('tile', 'blk'), may hold values from -6 to 6
- queries: bfloat16 [32, 16, 16, 2240], P('tile', 'blk'), may hold values from -12 to 12
- key_rows: bfloat16 [32, 16, 16, 2240], P('tile', 'blk'), may hold values from -12 to 12
- value_rows: bfloat16 [32, 16, 16, 2240], P('tile', 'blk'), may hold values from -12 to 12
- w_output: bfloat16 [2240, 2240], P('tile'), may hold values from -0.125 to 0.125
- w_inner: bfloat16 [2240, 2, 4096], P(None, None, 'tile'), may hold values from -0.125 to 0.125
- w_down: bfloat16 [4096, 2240], P('tile'), may hold values from -0.09375 to 0.09375
- spatial_taps: float32 [3, 3, 2, 4096], P(None, None, None, 'tile'), may hold values from -2 to 2
- temporal_taps: float32 [3, 2, 4096], P(None, None, 'tile'), may hold values from -3.5 to 3.5
Outputs:
- layer_out: bfloat16 [32, 16, 16, 2240], P('tile', 'blk')
All inputs are finite; a program needn't handle non-finite values.
Results may differ from a plain program's by a relative error of at most 0.009.
Values may be sent and summed in bfloat16 or wider, within the bound.
A program may use at most 128 MiB of HBM per device.

v0:
```python
import jax
import jax.numpy as jnp
from jax import lax
from jax.sharding import PartitionSpec as P

HEADS = 20
HEAD_DIM = 112
TAPS = 3


EPS = 1e-06


def from_partner(value, axis, stride):
    mask = 2**stride
    pairs = [(source, source ^ mask) for source in range(lax.axis_size(axis))]
    return lax.ppermute(value, axis, pairs)


def carried_in(x, axis, combine, identity):
    peers, position = (lax.axis_size(axis), lax.axis_index(axis))
    everything = jax.tree.map(lambda part: lax.all_gather(part, axis), x)
    start = jax.tree.map(
        lambda part, zero: jnp.broadcast_to(jnp.asarray(zero, part.dtype), part.shape), x, identity
    )

    def step(k, before):
        reached = k < position
        new = combine(before, jax.tree.map(lambda part: part[k], everything))
        return jax.tree.map(lambda a, b: jnp.where(reached, a, b), new, before)

    return lax.fori_loop(0, peers, step, start)


def shifted(x, axis, by):
    peers = lax.axis_size(axis)
    pairs = [(i, i + by) for i in range(peers) if 0 <= i + by < peers]
    return lax.ppermute(x, axis, pairs)


def add_pair(earlier, later):
    return (earlier[0] + later[0], earlier[1] + later[1])


def prefix_state(state_parts):
    partner = from_partner((state_parts[0], state_parts[1]), "blk", 0)
    block_sum = add_pair(state_parts, partner)
    odd_side = (lax.axis_index("blk") % 2).astype(jnp.float32)
    keep_share = 1.0 - 0.5 * odd_side
    zero_state = (jnp.zeros_like(block_sum[0]), jnp.zeros_like(block_sum[1]))
    before = carried_in((block_sum[0] * 0.5, block_sum[1] * 0.5), "blk", add_pair, zero_state)
    return (before[0] + block_sum[0] * keep_share, before[1] + block_sum[1] * keep_share)


def spatial_conv(inner_act, spatial_taps):
    row_count = inner_act.shape[0]
    col_count = inner_act.shape[2]
    padded = jnp.pad(inner_act, ((1, 1), (0, 0), (1, 1), (0, 0), (0, 0)))
    running = jnp.zeros(inner_act.shape, jnp.float32)
    for tap_row in range(3):
        for tap_col in range(3):
            window = padded[tap_row : tap_row + row_count, :, tap_col : tap_col + col_count]
            running = running + window.astype(jnp.float32) * spatial_taps[tap_row, tap_col]
    return running


def on_device(
    stream_in, queries, key_rows, value_rows, w_output, w_inner, w_down, spatial_taps, temporal_taps
):
    row_count, frames, col_count, model_width = queries.shape
    tokens = row_count * frames * col_count
    highest = lax.Precision.HIGHEST
    key_pos = jax.nn.relu(key_rows).reshape(tokens, HEADS, HEAD_DIM)
    value_heads = value_rows.reshape(tokens, HEADS, HEAD_DIM)
    local_kv = jnp.einsum("thd,the->hde", key_pos, value_heads, preferred_element_type=jnp.float32)
    local_kv = local_kv.reshape(model_width, HEAD_DIM)
    local_z = jnp.sum(key_pos.astype(jnp.float32), axis=0).reshape(model_width)
    shares = (
        lax.psum_scatter(local_kv, "tile", scatter_dimension=0, tiled=True),
        lax.psum_scatter(local_z, "tile", scatter_dimension=0, tiled=True),
    )
    share_state = prefix_state(shares)
    state, zsum = (
        lax.all_gather(share_state[0], "tile", axis=0, tiled=True),
        lax.all_gather(share_state[1], "tile", axis=0, tiled=True),
    )
    state = state.reshape(HEADS, HEAD_DIM, HEAD_DIM)
    zsum = zsum.reshape(HEADS, HEAD_DIM)
    query_pos = jax.nn.relu(queries.astype(jnp.float32)).reshape(tokens, HEADS, HEAD_DIM)
    numerator = jnp.einsum("thd,hde->the", query_pos, state, precision=highest)
    denominator = jnp.einsum("thd,hd->th", query_pos, zsum, precision=highest) + EPS
    attended = (numerator / denominator[..., None]).astype(jnp.bfloat16)
    attended = attended.reshape(row_count, frames, col_count, model_width)
    by_feature = lax.all_to_all(attended, "tile", split_axis=3, concat_axis=0, tiled=True)
    portion = by_feature
    product = jnp.dot(
        portion.reshape(-1, portion.shape[3]), w_output, preferred_element_type=jnp.float32
    )
    attn_out = lax.psum_scatter(
        product.reshape(row_count * lax.axis_size("tile"), frames, col_count, model_width),
        "tile",
        scatter_dimension=0,
        tiled=True,
    )
    hidden = (stream_in.astype(jnp.float32) + attn_out).astype(jnp.bfloat16)
    chan_dev = w_inner.shape[2]
    w_flat = w_inner.reshape(model_width, 2 * chan_dev)
    portion = lax.all_gather(hidden, "tile", axis=0, tiled=True)
    product = jnp.dot(portion.reshape(-1, model_width), w_flat, preferred_element_type=jnp.float32)
    activated = jax.nn.silu(product).astype(jnp.bfloat16)
    inner_act = activated.reshape(portion.shape[0], frames, col_count, 2, chan_dev)
    spatial = spatial_conv(inner_act, spatial_taps).astype(jnp.bfloat16)
    earlier_frames = shifted(spatial, "blk", 1)
    extended = jnp.concatenate([earlier_frames, spatial], axis=1)
    temporal_mix = jnp.zeros(spatial.shape, jnp.float32)
    for lag in range(TAPS):
        window = extended[:, TAPS - 1 - lag : TAPS - 1 - lag + frames]
        temporal_mix = temporal_mix + window.astype(jnp.float32) * temporal_taps[lag]
    gated_out = (temporal_mix[..., 0, :] * jax.nn.silu(temporal_mix[..., 1, :])).astype(
        jnp.bfloat16
    )
    portion = gated_out
    product = jnp.dot(portion.reshape(-1, chan_dev), w_down, preferred_element_type=jnp.float32)
    ffn_out = lax.psum_scatter(
        product.reshape(lax.axis_size("tile") * row_count, frames, col_count, model_width).astype(
            jnp.bfloat16
        ),
        "tile",
        scatter_dimension=0,
        tiled=True,
    ).astype(jnp.float32)
    return (hidden.astype(jnp.float32) + ffn_out).astype(jnp.bfloat16)


def solution(mesh):
    in_specs = (
        P("tile", "blk", None, None),
        P("tile", "blk", None, None),
        P("tile", "blk", None, None),
        P("tile", "blk", None, None),
        P("tile", None),
        P(None, None, "tile"),
        P("tile", None),
        P(None, None, None, "tile"),
        P(None, None, "tile"),
    )
    out_specs = P("tile", "blk", None, None)
    return jax.shard_map(
        on_device, mesh=mesh, in_specs=in_specs, out_specs=out_specs, check_vma=False
    )
```

profile of v0, /device:TPU:0, one launch (start us, length us, event | category | flops | bytes accessed | tf_op | source)
XLA Modules:
  0.0 571.9 jit_solution(4636084456415027600)
XLA Ops:
  6.5 2.5 broadcast_maximum_fusion
  9.1 4.0 reshape.58
  13.1 4.0 reshape.59
  17.1 3.5 fusion.8
  20.6 28.2 %reduce-scatter.4.cloned.1.call-done = f32[560,112]{1,0:T(8,128)} async-done(((f32[2240,112]{1,0:T(8,128)}), f32[560,112]{1,0:T(8,128)}) %reduce-scatter.4.cloned.1.call-update) | async-done | bytes 250896 | tf_op jit(solution)/shard_map/reduce_scatter | solution.py:79
  48.9 1.5 collective-permute-start
  50.3 7.2 %collective-permute-done = f32[560,112]{1,0:T(8,128)S(1)} collective-permute-done((f32[560,112]{1,0:T(8,128)}, f32[560,112]{1,0:T(8,128)S(1)}, u32[]{:S(2)}, u32[]{:S(2)}) %collective-permute-start) | collective-permute-done | bytes 250912 | tf_op jit(solution)/shard_map/ppermute | solution.py:17
  57.5 1.7 broadcast_multiply_fusion
  60.6 1.5 convert_reduce_fusion
  62.2 10.2 %all-reduce.3 = f32[2240]{0:T(1024)S(1)} all-reduce(f32[2240]{0:T(1024)S(1)} %convert_reduce_fusion), channel_id=5, replica_groups=mesh['blk'=8,'tile'=4] {'tile'}, use_global_device_ids=true, to_apply=%region_2.3.clone | all-reduce | flops 2240 | bytes 17920
  72.4 1.9 collective-permute-start.1
  74.3 3.0 convert_maximum_fusion
  79.2 4.3 reshape.62
  83.5 3.3 copy.27
  87.0 36.8 %all-reduce.1 = f32[4480]{0:T(1024)S(1)} all-reduce(f32[4480]{0:T(1024)S(1)} %multiply_dynamic-update-slice_fusion), channel_id=3, replica_groups=mesh['blk'=8,'tile'=4] {'blk'}, use_global_device_ids=true, to_apply=%add.1 | all-reduce | flops 4480 | bytes 35840
  123.9 8.9 %while.16 = (s32[]{:T(128)}, f32[560,112]{1,0:T(8,128)S(1)}, f32[560]{0:T(1024)S(1)}, s32[]{:T(128)}, f32[8,560,112]{2,1,0:T(8,128)}, /*index=5*/f32[8,560]{1,0:T(8,128)S(1)}, s32[]{:T(128)}, s32[]{:T(128)}) while((s32[]{:T(128)}, f32[560,112]{1,0:T(8,128)S(1)}, f32[560]{0:T(1024)S(1)}, s32[]{:T(128)}, f32[8,560,112]{2,1,0:T(8,128)}, ...), condition=%wide.region_4.5_spmd.clone, body=%wide.region_3.4_spmd.clone.sunk | while | flops 189844 | bytes 763955 | solution.py:32
  123.9 1.0 add_select_fusion.4
  125.0 1.0 add_select_fusion.4
  126.1 1.0 add_select_fusion.4
  127.3 1.0 add_select_fusion.4
  128.4 1.0 add_select_fusion.4
  129.5 1.0 add_select_fusion.4
  130.6 1.0 add_select_fusion.4
  131.7 1.0 add_select_fusion.4
  133.0 10.1 %all-reduce.2 = f32[2240]{0:T(1024)S(1)} all-reduce(f32[2240]{0:T(1024)S(1)} %add_dynamic-update-slice_fusion), channel_id=1, replica_groups=mesh['blk'=8,'tile'=4] {'tile'}, use_global_device_ids=true, to_apply=%add.2 | all-reduce | flops 2240 | bytes 17920
  143.2 3.0 fusion.14
  146.3 9.7 %all_gather.25 = f32[2240,112]{1,0:T(8,128)S(1)} all-gather(f32[560,112]{1,0:T(8,128)S(1)} %multiply_add_fusion.1), channel_id=1, replica_groups=mesh['blk'=8,'tile'=4] {'tile'}, dimensions={0}, use_global_device_ids=true | all-gather | bytes 1254400 | tf_op jit(solution)/shard_map/all_gather | solution.py:84
  156.0 3.2 fusion.5
  159.2 28.0 %reshape.86 = bf16[8,2,16,2240]{2,1,0,3:T(2,128)(2,1)} reshape(bf16[256,20,112]{0,2,1:T(8,128)(2,1)} %fusion.5) | data formatting | bytes 2293760 | tf_op jit(solution)/shard_map/reshape | solution.py:93
  187.2 11.8 %reshape.89 = bf16[4,2,71680]{2,1,0:T(2,128)(2,1)} reshape(bf16[2240,8,2,16]{3,2,1,0:T(2,128)(2,1)} %bitcast.90) | data formatting | bytes 2293760
  198.9 19.8 %all_to_all.15 = bf16[4,2,71680]{2,1,0:T(2,128)(2,1)} all-to-all(bf16[4,2,71680]{2,1,0:T(2,128)(2,1)} %reshape.89), channel_id=1, replica_groups=mesh['blk'=8,'tile'=4] {'tile'}, dimensions={0} | all-to-all | bytes 2293760 | tf_op jit(solution)/shard_map/all_to_all | solution.py:94
  218.8 8.7 %reshape.90 = bf16[2240,8,2,16]{3,2,1,0:T(2,128)(2,1)} reshape(bf16[4,2,71680]{2,1,0:T(2,128)(2,1)} %all_to_all.15) | data formatting | bytes 2293760
  227.5 19.9 %copy.30 = bf16[8,2,16,4,560]{4,2,1,0,3:T(8,128)(2,1)} copy(bf16[8,2,16,4,560]{2,1,0,4,3:T(2,128)(2,1)} %bitcast.91) | data formatting | bytes 2293760 | tf_op jit(solution)/shard_map/all_to_all | solution.py:94
  247.3 7.8 %fusion.3 = f32[32,2,16,2240]{3,2,1,0:T(8,128)} fusion(bf16[32,2,16,560]{3,2,1,0:T(8,128)(2,1)} %bitcast.95, bf16[560,2240]{1,0:T(8,128)(2,1)S(1)} %copy-done), kind=kOutput, calls=%fused_computation.21 | convolution fusion | flops 2569011200 | bytes 12830720 | tf_op jit(solution)/shard_map/dot_general | solution.py:96
  255.2 74.2 %reduce-scatter.6.cloned.1.call-done = f32[8,2,16,2240]{3,2,1,0:T(8,128)} async-done(((f32[32,2,16,2240]{3,2,1,0:T(8,128)}), f32[8,2,16,2240]{3,2,1,0:T(8,128)}) %reduce-scatter.6.cloned.1.call-update) | async-done | bytes 2293776 | tf_op jit(solution)/shard_map/reduce_scatter | solution.py:99
  329.4 2.9 add_convert_fusion.2
  332.6 11.4 %copy.38 = bf16[280,8,2,1024]{3,1,2,0:T(8,128)(2,1)} copy(bf16[280,8,2,1024]{3,2,1,0:T(2,128)(2,1)} %bitcast.92) | data formatting | bytes 18350080
  344.1 25.9 %all-gather.5.cloned.1.call-done = bf16[32,2,16,2240]{3,2,1,0:T(8,128)(2,1)} async-done(((bf16[8,2,16,2240]{3,2,1,0:T(8,128)(2,1)}), bf16[32,2,16,2240]{3,2,1,0:T(8,128)(2,1)}) %all-gather.5.cloned.1.call-update) | async-done | bytes 4587536 | tf_op jit(solution)/shard_map/all_gather | solution.py:108
  370.0 16.0 %multiply_convert_fusion = bf16[1024,2048]{1,0:T(8,128)(2,1)} fusion(bf16[1024,2240]{1,0:T(8,128)(2,1)} %bitcast.98, bf16[2240,2048]{1,0:T(8,128)(2,1)} %bitcast.93), kind=kOutput, calls=%fused_computation.13 | convolution fusion | flops 9405726720 | bytes 17956864 | tf_op jit(solution)/shard_map/dot_general | solution.py:109
  386.0 7.8 %reshape.67 = bf16[32,2,16,2,1024]{4,3,2,1,0:T(2,128)(2,1)} reshape(bf16[1024,2048]{1,0:T(8,128)(2,1)} %multiply_convert_fusion) | data formatting | bytes 8388608 | tf_op jit(solution)/shard_map/reshape | solution.py:111
  393.8 3.5 copy.31
  397.3 11.9 %add_convert_fusion = bf16[32,2,16,2,1024]{4,2,1,0,3:T(8,128)(2,1)S(1)} fusion(bf16[32,2,16,2,1024]{4,2,1,0,3:T(8,128)(2,1)S(1)} %copy.31, f32[2,1024]{1,0:T(2,128)S(1)} %get-tuple-element.157, f32[2,1024]{1,0:T(2,128)S(1)} %get-tuple-element.158, f32[2,1024]{1,0:T(2,128)S(1)} %get-tuple-element.151, f32[2,1024]{1,0:T(2,128)S(1)} %get-tuple-element.152, ...), kind=kLoop, calls=%fused_computation.12 | loop fusion | flops 56623104 | bytes 8462336 | tf_op jit(solution)/shard_map/convert_element_type | solution.py:112
  409.2 3.9 collective-permute-start.2
  413.2 89.7 %collective-permute-done.2 = bf16[32,2,16,2,1024]{4,2,1,0,3:T(8,128)(2,1)S(1)} collective-permute-done((bf16[32,2,16,2,1024]{4,2,1,0,3:T(8,128)(2,1)S(1)}, bf16[32,2,16,2,1024]{4,2,1,0,3:T(8,128)(2,1)S(1)}, u32[]{:S(2)}, u32[]{:S(2)}) %collective-permute-start.2) | collective-permute-done | bytes 4194336 | tf_op jit(solution)/shard_map/ppermute | solution.py:38
  502.8 3.2 multiply_add_fusion
  506.0 7.3 %convolution_convert_fusion = bf16[32,2,16,2240]{3,2,1,0:T(8,128)(2,1)} fusion(bf16[1024,2240]{0,1:T(8,128)(2,1)S(1)} %bitcast.100, f32[32,2,16,2,1024]{4,2,1,0,3:T(8,128)S(1)} %multiply_add_fusion), kind=kOutput, calls=%fused_computation.14 | convolution fusion | flops 4706205696 | bytes 17563648 | tf_op jit(solution)/shard_map/dot_general | solution.py:123
  513.4 49.1 %reduce-scatter.8.cloned.1.call-done = bf16[8,2,16,2240]{3,2,1,0:T(8,128)(2,1)} async-done(((bf16[32,2,16,2240]{3,2,1,0:T(8,128)(2,1)}), bf16[8,2,16,2240]{3,2,1,0:T(8,128)(2,1)}) %reduce-scatter.8.cloned.1.call-update) | async-done | bytes 1146896 | tf_op jit(solution)/shard_map/reduce_scatter | solution.py:124
  562.5 2.9 add_convert_fusion.1
  (66 shorter events, 2.8 us)
Async XLA Ops:
  6.5 240.8 %copy-start = (bf16[560,2240]{1,0:T(8,128)(2,1)S(1)}, bf16[560,2240]{1,0:T(8,128)(2,1)}, u32[]{:S(2)}) copy-start(bf16[560,2240]{1,0:T(8,128)(2,1)} %param.15) | copy-start | bytes 7526404
  6.5 42.3 %reduce-scatter.4.cloned.1.call-start = ((), (), s32[]{:S(2)}) async-start(), calls=%async_computation.4 | async-start | bytes 1433600 | tf_op jit(solution)/shard_map/reduce_scatter | solution.py:79
  13.1 46.2 %copy-start.7 = (u32[32]{0:T(128)S(1)}, u32[32]{0:T(128)}, u32[]{:S(2)}) copy-start(u32[32]{0:T(128)} %constant.77) | copy-start | bytes 388
  20.6 56.7 %copy-start.8 = (u32[32]{0:T(128)S(1)}, u32[32]{0:T(128)}, u32[]{:S(2)}) copy-start(u32[32]{0:T(128)} %constant.72) | copy-start | bytes 388
  20.6 103.3 %all-gather.7.cloned.1.call-start = ((), (), s32[]{:S(2)}) async-start(), calls=%async_computation.8 | async-start | bytes 2580480 | tf_op jit(solution)/shard_map/all_gather | solution.py:22
  48.9 8.6 %collective-permute-start = (f32[560,112]{1,0:T(8,128)}, f32[560,112]{1,0:T(8,128)S(1)}, u32[]{:S(2)}, u32[]{:S(2)}) collective-permute-start(f32[560,112]{1,0:T(8,128)} %reduce-scatter.4.cloned.1.call-done), channel_id=1, source_target_pairs={{0,4},{4,0},{8,12},{12,8},{16,20},{20,16},{24,28},{28,24},{1,5},{5... | collective-permute-start | bytes 752648 | tf_op jit(solution)/shard_map/ppermute | solution.py:17
  59.3 270.2 %reduce-scatter.6.cloned.1.call-start = ((), (), s32[]{:S(2)}) async-start(), calls=%async_computation.5 | async-start | bytes 11796480 | tf_op jit(solution)/shard_map/reduce_scatter | solution.py:99
  72.4 14.4 %collective-permute-start.1 = (f32[560]{0:T(1024)S(1)}, f32[560]{0:T(1024)S(1)}, u32[]{:S(2)}, u32[]{:S(2)}) collective-permute-start(f32[560]{0:T(1024)S(1)} %dynamic-slice.3), channel_id=1, source_target_pairs={{0,4},{4,0},{8,12},{12,8},{16,20},{20,16},{24,28},{28,24},{1,5},{5... | collective-permute-start | bytes 6728 | tf_op jit(solution)/shard_map/ppermute | solution.py:17
  86.8 59.4 %copy-start.4 = (f32[560,112]{1,0:T(8,128)S(1)}, f32[560,112]{1,0:T(8,128)}, u32[]{:S(2)}) copy-start(f32[560,112]{1,0:T(8,128)} %reduce-scatter.4.cloned.1.call-done) | copy-start | bytes 752644
  143.2 12.8 %copy-start.2 = (f32[256,20,112]{0,2,1:T(8,128)S(1)}, f32[256,20,112]{0,2,1:T(8,128)}, u32[]{:S(2)}) copy-start(f32[256,20,112]{0,2,1:T(8,128)} %copy.27) | copy-start | bytes 6881284
  255.2 74.3 %copy-start.3 = (bf16[8,2,16,2240]{3,2,1,0:T(8,128)(2,1)S(1)}, bf16[8,2,16,2240]{3,2,1,0:T(8,128)(2,1)}, u32[]{:S(2)}) copy-start(bf16[8,2,16,2240]{3,2,1,0:T(8,128)(2,1)} %param.11) | copy-start | bytes 3440644
  255.2 114.8 %all-gather.5.cloned.1.call-start = ((), (), s32[]{:S(2)}) async-start(), calls=%async_computation.6 | async-start | bytes 5898240 | tf_op jit(solution)/shard_map/all_gather | solution.py:108
  332.4 230.1 %reduce-scatter.8.cloned.1.call-start = ((), (), s32[]{:S(2)}) async-start(), calls=%async_computation.7 | async-start | bytes 5898240 | tf_op jit(solution)/shard_map/reduce_scatter | solution.py:124
  332.6 11.4 %copy-start.5 = (f32[3,3,2,1024]{3,2,1,0:T(2,128)S(1)}, f32[3,3,2,1024]{3,2,1,0:T(2,128)}, u32[]{:S(2)}) copy-start(f32[3,3,2,1024]{3,2,1,0:T(2,128)} %param.18) | copy-start | bytes 221188
  397.3 15.8 %copy-start.6 = (f32[3,2,1024]{2,1,0:T(2,128)S(1)}, f32[3,2,1024]{2,1,0:T(2,128)}, u32[]{:S(2)}) copy-start(f32[3,2,1024]{2,1,0:T(2,128)} %param.19) | copy-start | bytes 73732
  397.3 108.7 %slice-start = ((s8[4587520]{0:T(1024)(128)(4,1)}), s8[4194304]{0:T(1024)(128)(4,1)S(1)}, s32[]{:S(2)}) async-start(s8[4587520]{0:T(1024)(128)(4,1)} %bitcast.99), calls=%async_computation.9 | async-start | bytes 8388608
  409.2 93.6 %collective-permute-start.2 = (bf16[32,2,16,2,1024]{4,2,1,0,3:T(8,128)(2,1)S(1)}, bf16[32,2,16,2,1024]{4,2,1,0,3:T(8,128)(2,1)S(1)}, u32[]{:S(2)}, u32[]{:S(2)}) collective-permute-start(bf16[32,2,16,2,1024]{4,2,1,0,3:T(8,128)(2,1)S(1)} %add_convert_fusion), channel_id=1, source_target_pairs={{0,4},{4,8},{8,12},{12,16},{16,20},{20,24},{24,28},{1,5},{5,9},{9,... | collective-permute-start | bytes 12582920 | tf_op jit(solution)/shard_map/ppermute | solution.py:38
  502.8 3.2 slice-start.1
  506.0 59.4 %copy-start.1 = (bf16[560,2240]{1,0:T(8,128)(2,1)S(1)}, bf16[560,2240]{1,0:T(8,128)(2,1)}, u32[]{:S(2)}) copy-start(bf16[560,2240]{1,0:T(8,128)(2,1)} %param.15) | copy-start | bytes 7526404
Sparse Core Ops, SparseCore 0:
  20.7 28.1 reduce-scatter.3
  59.4 51.7 all-gather.6
  255.3 74.0 reduce-scatter.5
  332.5 37.4 all-gather.4
  513.5 48.9 reduce-scatter.7
where the time goes:
time: 574 us; the launch traced here: 572 us
  waiting for transfers between devices  274 us (48%)
  local copies, waits for them, and re-layouts  108 us (19%)
  blocking collectives  86.6 us (15%)
  matrix products  40.7 us (7%)
  other arithmetic  38.5 us (7%)
  between operations  15.2 us (3%)
  starting transfers between devices  7.66 us (1%)
    ppermute x1, waiting for transfers between devices, shifted(): return lax.ppermute(x, axis, pairs)  89.7 us
    reduce_scatter x1, waiting for transfers between devices, on_device(): lax.psum_scatter(product.reshape(row_count * lax.axis_size('tile'), frame...  74.2 us
    unnamed x3, blocking collectives  57.1 us
    reduce_scatter x1, waiting for transfers between devices, on_device(): lax.psum_scatter(product.reshape(lax.axis_size('tile') * row_count, frame...  49.1 us
    unnamed x30, local copies, waits for them, and re-layouts  33.3 us
    reduce_scatter x1, waiting for transfers between devices, on_device(): lax.psum_scatter(local_kv, 'tile', scatter_dimension=0, tiled=True)  28.2 us
    reshape x1, local copies, waits for them, and re-layouts, on_device(): attended = attended.reshape(row_count, frames, col_count, model_width)  28 us
    all_gather x1, waiting for transfers between devices, on_device(): portion = lax.all_gather(hidden, 'tile', axis=0, tiled=True)  25.9 us
  transfers between devices with their start and end apart: 8, of which 6 were waited for; matrix products, arithmetic and copies ran while one was open for 4% of the time, Pallas kernels for 0%

commit v1 on v0

v1 whole, which is shorter than its diff:
```python
import functools

import jax
import jax.numpy as jnp
from jax import lax
from jax.experimental import pallas as pl
from jax.experimental.pallas import tpu as pltpu
from jax.sharding import PartitionSpec as P

HEADS = 20
HEAD_DIM = 112
TAPS = 3
BLOCK_F = 4
LANES = 128
EPS = 1e-06

MESH = pl.DeviceIdType.MESH


def vmem_specs(count):
    return [pl.BlockSpec(memory_space=pltpu.VMEM)] * count


def shifted(x, axis, by):
    peers = lax.axis_size(axis)
    pairs = [(i, i + by) for i in range(peers) if 0 <= i + by < peers]
    return lax.ppermute(x, axis, pairs)


def head_columns(head):
    return slice(head * HEAD_DIM, (head + 1) * HEAD_DIM)


def local_state_kernel(key_ref, value_ref, kv_ref):
    tokens = key_ref.shape[0]
    ones = jnp.ones((tokens, LANES - HEAD_DIM), jnp.bfloat16)
    for head in range(HEADS):
        keys = jnp.maximum(key_ref[:, head_columns(head)], 0)
        values = jnp.concatenate([value_ref[:, head_columns(head)], ones], axis=1)
        kv = lax.dot_general(
            keys, values, (((0,), (0,)), ((), ())), preferred_element_type=jnp.float32
        )
        kv_ref[head] = kv.astype(jnp.bfloat16)
    for head in range(HEADS, kv_ref.shape[0]):
        kv_ref[head] = jnp.zeros(kv_ref.shape[1:], jnp.bfloat16)


def exchange_kernel(
    blocks, pair, tiles, kv_ref, state_ref, got1, got2, total, block_send, final_send, states,
    send1, recv1, send2, recv2, send3, recv3,
):
    group = pair * tiles
    blk = lax.axis_index("blk")
    tile = lax.axis_index("tile")
    block = blk // pair
    member = blk % pair
    rank = member * tiles + tile

    def peer(step):
        other = (rank + step) % group
        return other, (block * pair + other // tiles, other % tiles)

    barrier = pltpu.get_barrier_semaphore()
    for step in range(1, group):
        pl.semaphore_signal(barrier, inc=1, device_id=peer(step)[1], device_id_type=MESH)
    for step in range(1, blocks):
        other = (block + step) % blocks
        pl.semaphore_signal(
            barrier, inc=1, device_id=(other * pair + member, tile), device_id_type=MESH
        )
    pl.semaphore_wait(barrier, group - 1 + blocks - 1)

    first = []
    for step in range(1, group):
        other, device = peer(step)
        copy = pltpu.make_async_remote_copy(
            src_ref=kv_ref.at[other], dst_ref=got1.at[step], send_sem=send1.at[step],
            recv_sem=recv1.at[step], device_id=device, device_id_type=MESH,
        )
        copy.start()
        first.append(copy)
    total[...] = kv_ref[rank].astype(jnp.float32)
    for step in range(1, group):
        first[step - 1].wait_recv()
        total[...] += got1[step].astype(jnp.float32)

    block_send[...] = total[...].astype(jnp.bfloat16)

    def later(step):
        return pltpu.make_async_remote_copy(
            src_ref=block_send, dst_ref=got2.at[step], send_sem=send2.at[step],
            recv_sem=recv2.at[step], device_id=(((block + step) % blocks) * pair + member, tile),
            device_id_type=MESH,
        )

    for step in range(1, blocks):

        @pl.when(block + step < blocks)
        def _():
            later(step).start()

    for step in range(1, blocks):

        @pl.when(block >= step)
        def _():
            later(step).wait_recv()
            total[...] += got2[step].astype(jnp.float32)

    final_send[...] = total[...].astype(jnp.bfloat16)
    third = []
    for step in range(1, group):
        copy = pltpu.make_async_remote_copy(
            src_ref=final_send, dst_ref=states.at[rank], send_sem=send3.at[step],
            recv_sem=recv3.at[step], device_id=peer(step)[1], device_id_type=MESH,
        )
        copy.start()
        third.append(copy)
    state_ref[rank] = total[...].astype(jnp.bfloat16)
    for step in range(1, group):
        third[step - 1].wait_recv()
        other = (rank + group - step) % group
        state_ref[other] = states[other]
    for step in range(1, group):
        first[step - 1].wait_send()
        third[step - 1].wait_send()
    for step in range(1, blocks):

        @pl.when(block + step < blocks)
        def _():
            later(step).wait_send()


def exchange_states(kv, blocks, pair, tiles):
    group = pair * tiles
    piece = kv.shape[1:]
    dma = pltpu.SemaphoreType.DMA
    return pl.pallas_call(
        functools.partial(exchange_kernel, blocks, pair, tiles),
        out_shape=jax.ShapeDtypeStruct(kv.shape, jnp.bfloat16),
        in_specs=vmem_specs(1),
        out_specs=vmem_specs(1)[0],
        scratch_shapes=[
            pltpu.VMEM((group,) + piece, jnp.bfloat16),
            pltpu.VMEM((blocks,) + piece, jnp.bfloat16),
            pltpu.VMEM(piece, jnp.float32),
            pltpu.VMEM(piece, jnp.bfloat16),
            pltpu.VMEM(piece, jnp.bfloat16),
            pltpu.VMEM((group,) + piece, jnp.bfloat16),
            dma((group,)),
            dma((group,)),
            dma((blocks,)),
            dma((blocks,)),
            dma((group,)),
            dma((group,)),
        ],
        compiler_params=pltpu.CompilerParams(collective_id=0, has_side_effects=True),
    )(kv)


def attention_kernel(query_ref, state_ref, out_ref):
    for head in range(HEADS):
        queries = jnp.maximum(query_ref[:, head_columns(head)], 0)
        both = jnp.dot(queries, state_ref[head], preferred_element_type=jnp.float32)
        ratio = both[:, :HEAD_DIM] / (both[:, HEAD_DIM : HEAD_DIM + 1] + EPS)
        out_ref[:, head_columns(head)] = ratio.astype(jnp.bfloat16)


def column_masks(stride, cols, width):
    col = lax.broadcasted_iota(jnp.int32, (stride, width), 0) % cols
    return col > 0, col < cols - 1


def fill_inner(hidden_ref, w_ref, inner, stride, chunk):
    tokens = hidden_ref.shape[0]
    edge = jnp.zeros((stride, inner.shape[1]), jnp.bfloat16)
    inner[:stride] = edge
    inner[stride + tokens :] = edge
    for start in range(0, tokens, chunk):
        product = jnp.dot(
            hidden_ref[start : start + chunk], w_ref[...], preferred_element_type=jnp.float32
        )
        inner[stride + start : stride + start + chunk] = jax.nn.silu(product).astype(jnp.bfloat16)


def conv_row(inner, taps_ref, row, stride, masks):
    rows = [
        inner[pl.ds(pl.multiple_of((row + a) * stride, stride), stride)].astype(jnp.float32)
        for a in range(3)
    ]
    sums = [
        sum(rows[a] * taps_ref[3 * a + b : 3 * a + b + 1] for a in range(3)) for b in range(3)
    ]
    from_left = jnp.where(masks[0], pltpu.roll(sums[0], 1, 0), 0.0)
    from_right = jnp.where(masks[1], pltpu.roll(sums[2], stride - 1, 0), 0.0)
    return sums[1] + from_left + from_right


def spatial_kernel(stride, cols, chunk, hidden_ref, w_ref, taps_ref, out_ref, inner):
    fill_inner(hidden_ref, w_ref, inner, stride, chunk)
    masks = column_masks(stride, cols, inner.shape[1])

    def body(row, carry):
        value = conv_row(inner, taps_ref, row, stride, masks)
        out_ref[pl.ds(pl.multiple_of(row * stride, stride), stride)] = value.astype(jnp.bfloat16)
        return carry

    lax.fori_loop(0, hidden_ref.shape[0] // stride, body, 0, unroll=2)


def gated_kernel(
    stride, cols, chunk, hidden_ref, wv_ref, wg_ref, sv_ref, sg_ref, tv_ref, tg_ref, ov_ref, og_ref,
    out_ref, inner_v, inner_g,
):
    fill_inner(hidden_ref, wv_ref, inner_v, stride, chunk)
    fill_inner(hidden_ref, wg_ref, inner_g, stride, chunk)
    masks = column_masks(stride, cols, inner_v.shape[1])

    def mixed(inner, taps_ref, time_ref, own_ref, row, where):
        before = conv_row(inner, taps_ref, row, stride, masks)
        before = before.astype(jnp.bfloat16).astype(jnp.float32)
        extended = jnp.concatenate([before, own_ref[where].astype(jnp.float32)], axis=0)
        total = extended[stride:] * time_ref[0:1]
        for lag in range(1, TAPS):
            start = stride - lag * cols
            total = total + extended[start : start + stride] * time_ref[lag : lag + 1]
        return total

    def body(row, carry):
        where = pl.ds(pl.multiple_of(row * stride, stride), stride)
        value = mixed(inner_v, sv_ref, tv_ref, ov_ref, row, where)
        gate = mixed(inner_g, sg_ref, tg_ref, og_ref, row, where)
        out_ref[where] = (value * jax.nn.silu(gate)).astype(jnp.bfloat16)
        return carry

    lax.fori_loop(0, hidden_ref.shape[0] // stride, body, 0)


def on_device(
    stream_in, queries, key_rows, value_rows, w_output, w_inner, w_down, spatial_taps, temporal_taps
):
    row_count, frames, col_count, width = queries.shape
    tokens = row_count * frames * col_count
    tiles = lax.axis_size("tile")
    pair = BLOCK_F // frames
    blocks = lax.axis_size("blk") // pair
    group = pair * tiles
    per_rank = -(-HEADS // group)
    bf16 = jnp.bfloat16

    w_full = lax.all_gather(w_output, "tile", axis=0, tiled=True)

    kv = pl.pallas_call(
        local_state_kernel,
        out_shape=jax.ShapeDtypeStruct((group * per_rank, HEAD_DIM, LANES), bf16),
        in_specs=vmem_specs(2),
        out_specs=vmem_specs(1)[0],
    )(key_rows.reshape(tokens, width), value_rows.reshape(tokens, width))
    state = exchange_states(
        kv.reshape(group, per_rank, HEAD_DIM, LANES), blocks, pair, tiles
    ).reshape(group * per_rank, HEAD_DIM, LANES)
    attended = pl.pallas_call(
        attention_kernel,
        out_shape=jax.ShapeDtypeStruct((tokens, width), bf16),
        in_specs=vmem_specs(2),
        out_specs=vmem_specs(1)[0],
    )(queries.reshape(tokens, width), state)

    attn_out = jnp.dot(attended, w_full, preferred_element_type=jnp.float32)
    hidden = (stream_in.reshape(tokens, width).astype(jnp.float32) + attn_out).astype(bf16)

    chan = w_inner.shape[2]
    w_flat = w_inner.reshape(width, 2 * chan)
    space = spatial_taps.reshape(9, 2 * chan)
    time = temporal_taps.reshape(TAPS, 2 * chan)
    before = shifted(hidden, "blk", 1)
    own_all = lax.all_gather(hidden, "tile", axis=0, tiled=True)
    before_all = lax.all_gather(before, "tile", axis=0, tiled=True)

    whole = tokens * tiles
    stride = frames * col_count
    lane_block = 256
    chunk = 256
    value_blocks = chan // lane_block
    full = lambda rows: pl.BlockSpec((rows, width), lambda j: (0, 0))
    block = lambda rows: pl.BlockSpec((rows, lane_block), lambda j: (0, j))
    gate = lambda rows: pl.BlockSpec((rows, lane_block), lambda j: (0, j + value_blocks))
    inner_scratch = pltpu.VMEM((whole + 2 * stride, lane_block), bf16)
    flops = 2 * whole * width * 2 * chan
    cost = pl.CostEstimate(
        flops=flops, bytes_accessed=2 * (whole * width + 2 * width * chan), transcendentals=0
    )
    spatial = pl.pallas_call(
        functools.partial(spatial_kernel, stride, col_count, chunk),
        grid=(2 * value_blocks,),
        out_shape=jax.ShapeDtypeStruct((whole, 2 * chan), bf16),
        in_specs=[full(whole), block(width), block(9)],
        out_specs=block(whole),
        scratch_shapes=[inner_scratch],
        cost_estimate=cost,
        compiler_params=pltpu.CompilerParams(vmem_limit_bytes=40 * 2**20),
    )(own_all, w_flat, space)
    gated_out = pl.pallas_call(
        functools.partial(gated_kernel, stride, col_count, chunk),
        grid=(value_blocks,),
        out_shape=jax.ShapeDtypeStruct((whole, chan), bf16),
        in_specs=[
            full(whole), block(width), gate(width), block(9), gate(9), block(TAPS), gate(TAPS),
            block(whole), gate(whole),
        ],
        out_specs=block(whole),
        scratch_shapes=[inner_scratch, inner_scratch],
        cost_estimate=cost,
        compiler_params=pltpu.CompilerParams(vmem_limit_bytes=48 * 2**20),
    )(before_all, w_flat, w_flat, space, space, time, time, spatial, spatial)

    product = jnp.dot(gated_out, w_down, preferred_element_type=jnp.float32).astype(bf16)
    ffn_out = lax.psum_scatter(product, "tile", scatter_dimension=0, tiled=True)
    layer_out = (hidden.astype(jnp.float32) + ffn_out.astype(jnp.float32)).astype(bf16)
    return layer_out.reshape(queries.shape)


def solution(mesh):
    in_specs = (
        P("tile", "blk", None, None),
        P("tile", "blk", None, None),
        P("tile", "blk", None, None),
        P("tile", "blk", None, None),
        P("tile", None),
        P(None, None, "tile"),
        P("tile", None),
        P(None, None, None, "tile"),
        P(None, None, "tile"),
    )
    out_specs = P("tile", "blk", None, None)
    return jax.shard_map(
        on_device, mesh=mesh, in_specs=in_specs, out_specs=out_specs, check_vma=False
    )
```

time: 574 us -> 275 us (0.48)
  waiting for transfers between devices: 274 us -> 125 us
  blocking collectives: 86.6 us -> 0 us
  Pallas kernels: 0 us -> 86.4 us
  local copies, waits for them, and re-layouts: 108 us -> 25.7 us
  other arithmetic: 38.5 us -> 2.55 us
  matrix products: 40.7 us -> 17.3 us
    reduce_scatter x3 -> x1, waiting for transfers between devices: 152 us -> 48.1 us  [on_device(): ffn_out = lax.psum_scatter(product, 'tile', scatter_dimension=0, tiled=True)]
    pallas_call x0 -> x5, Pallas kernels: none -> 86.4 us  [the longest x1 28.3 us: exchange_states(): pl.pallas_call(functools.partial(exchange_kernel, blocks, pair, tiles), o...]
    ppermute x1, waiting for transfers between devices: 89.7 us -> 24.8 us  [shifted(): return lax.ppermute(x, axis, pairs)]
    unnamed x3 -> x0, blocking collectives: 57.1 us -> none
    reshape x8 -> x0, local copies, waits for them, and re-layouts: 55.1 us -> none  [the longest x1 28 us: on_device(): attended = attended.reshape(row_count, frames, col_count, model_width)]
    all_gather x2 -> x3, waiting for transfers between devices: 25.9 us -> 51.5 us  [the longest x1 44.7 us: on_device(): w_full = lax.all_gather(w_output, 'tile', axis=0, tiled=True)]
    dot_general x6 -> x2, matrix products: 40.7 us -> 17.3 us  [the longest x1 9.01 us: on_device(): jnp.dot(gated_out, w_down, preferred_element_type=jnp.float32).astype(bf16)]
    all_to_all x1 -> x0, local copies, waits for them, and re-layouts: 19.9 us -> none  [on_device(): lax.all_to_all(attended, 'tile', split_axis=3, concat_axis=0, tiled=True)]
  transfers between devices with their start and end apart: 8 -> 5, of which waited for: 6 -> 4; matrix products, arithmetic and copies ran while one was open for 4% -> 5% of each run, Pallas kernels for 0% -> 22%
where the time goes in v1:
time: 275 us; the launch traced here: 274 us
  waiting for transfers between devices  125 us (45%)
  Pallas kernels  86.4 us (31%)
  local copies, waits for them, and re-layouts  25.7 us (9%)
  matrix products  17.3 us (6%)
  between operations  13.2 us (5%)
  starting transfers between devices  3.74 us (1%)
    reduce_scatter x1, waiting for transfers between devices, on_device(): ffn_out = lax.psum_scatter(product, 'tile', scatter_dimension=0, tiled=True)  48.1 us
    all_gather x1, waiting for transfers between devices, on_device(): w_full = lax.all_gather(w_output, 'tile', axis=0, tiled=True)  44.7 us
    pallas_call x1, Pallas kernels, exchange_states(): pl.pallas_call(functools.partial(exchange_kernel, blocks, pair, tiles), o...  28.3 us
    ppermute x1, waiting for transfers between devices, shifted(): return lax.ppermute(x, axis, pairs)  24.8 us
    pallas_call x1, Pallas kernels, on_device(): pl.pallas_call(functools.partial(gated_kernel, stride, col_count, chunk),...  24.8 us
    pallas_call x1, Pallas kernels, on_device(): pl.pallas_call(functools.partial(spatial_kernel, stride, col_count, chunk...  21.3 us
    unnamed x16, local copies, waits for them, and re-layouts  15.9 us
    dot_general x1, matrix products, on_device(): jnp.dot(gated_out, w_down, preferred_element_type=jnp.float32).astype(bf16)  9.01 us
  transfers between devices with their start and end apart: 5, of which 4 were waited for; matrix products, arithmetic and copies ran while one was open for 5% of the time, Pallas kernels for 22%

profile of v1, /device:TPU:0, one launch (start us, length us, event | category | flops | bytes accessed | tf_op | source)
XLA Modules:
  0.0 274.2 jit_solution(548587765772193568)
XLA Ops:
  6.5 0.0 all-gather.4.cloned.1.call-start
  6.5 0.7 all-gather.4.cloned.1.call-update
  7.3 0.0 all-gather.8.cloned.1.call-start
  7.3 4.9 %shard_map.91 = bf16[24,112,128]{2,1,0:T(8,128)(2,1)} custom-call(bf16[256,2240]{1,0:T(8,128)(2,1)} %bitcast.31, bf16[256,2240]{1,0:T(8,128)(2,1)} %bitcast.32), custom_call_target="tpu_custom_call" | custom-call | tf_op jit(solution)/shard_map/pallas_call | solution.py:252
  12.2 0.0 copy-start.5
  12.2 28.3 %shard_map.92 = bf16[8,3,112,128]{3,2,1,0:T(8,128)(2,1)} custom-call(bf16[8,3,112,128]{3,2,1,0:T(8,128)(2,1)} %bitcast.30), custom_call_target="tpu_custom_call" | custom-call | tf_op jit(solution)/shard_map/pallas_call | solution.py:137
  40.5 7.1 %shard_map.93 = bf16[256,2240]{1,0:T(8,128)(2,1)} custom-call(bf16[256,2240]{1,0:T(8,128)(2,1)} %bitcast.33, bf16[24,112,128]{2,1,0:T(8,128)(2,1)} %bitcast.29), custom_call_target="tpu_custom_call" | custom-call | tf_op jit(solution)/shard_map/pallas_call | solution.py:261
  47.6 44.7 %all-gather.4.cloned.1.call-done = bf16[2240,2240]{1,0:T(8,128)(2,1)} async-done(((bf16[560,2240]{1,0:T(8,128)(2,1)}), bf16[2240,2240]{1,0:T(8,128)(2,1)}) %all-gather.4.cloned.1.call-update) | async-done | bytes 10035216 | tf_op jit(solution)/shard_map/all_gather | solution.py:250
  92.3 0.0 copy-done.5
  92.3 8.3 %fusion = bf16[256,2240]{1,0:T(8,128)(2,1)} fusion(bf16[256,2240]{1,0:T(8,128)(2,1)} %shard_map.93, bf16[2240,2240]{1,0:T(8,128)(2,1)} %all-gather.4.cloned.1.call-done, bf16[256,2240]{1,0:T(8,128)(2,1)S(1)} %bitcast.37), kind=kOutput, calls=%fused_computation.2 | convolution fusion | flops 2570731520 | bytes 13475840 | tf_op jit(solution)/shard_map/dot_general | solution.py:268
  100.6 0.0 all-gather.8.cloned.1.call-update
  100.6 0.0 all-gather.6.cloned.1.call-start
  100.7 1.7 copy.17
  102.4 3.4 %collective-permute-start = (bf16[256,2240]{0,1:T(8,128)(2,1)S(1)}, bf16[256,2240]{0,1:T(8,128)(2,1)S(1)}, u32[]{:S(2)}, u32[]{:S(2)}) collective-permute-start(bf16[256,2240]{0,1:T(8,128)(2,1)S(1)} %copy.17), channel_id=1, source_target_pairs={{0,4},{4,8},{8,12},{12,16},{16,20},{20,24},{24,28},{1,5},{5,9},{9,... | collective-permute-start | bytes 3440648 | tf_op jit(solution)/shard_map/ppermute | solution.py:27
  105.8 24.8 %collective-permute-done = bf16[256,2240]{0,1:T(8,128)(2,1)S(1)} collective-permute-done((bf16[256,2240]{0,1:T(8,128)(2,1)S(1)}, bf16[256,2240]{0,1:T(8,128)(2,1)S(1)}, u32[]{:S(2)}, u32[]{:S(2)}) %collective-permute-start) | collective-permute-done | bytes 1146912 | tf_op jit(solution)/shard_map/ppermute | solution.py:27
  130.7 1.5 copy.18
  132.2 0.0 all-gather.6.cloned.1.call-update
  132.2 0.2 reduce-scatter.2.cloned.1.call-start
  132.4 0.0 copy-start.3
  132.5 0.0 copy-start.4
  132.5 11.1 %copy.21 = bf16[280,8,2,1024]{3,1,2,0:T(8,128)(2,1)} copy(bf16[280,8,2,1024]{3,2,1,0:T(2,128)(2,1)} %bitcast.25) | data formatting | bytes 18350080
  143.6 0.0 copy-done.3
  143.7 0.0 copy-done.4
  143.7 0.0 all-gather.8.cloned.1.call-done.hidden_ref
  143.7 0.0 copy-start
  143.7 2.7 copy-done
  146.5 21.3 %shard_map.94.ov_ref.og_ref = bf16[1024,2048]{1,0:T(8,128)(2,1)S(1)} custom-call(bf16[1024,2240]{1,0:T(8,128)(2,1)S(1)} %copy-done, bf16[2240,2048]{1,0:T(8,128)(2,1)} %bitcast.26, f32[9,2048]{1,0:T(8,128)S(1)} %bitcast.20), custom_call_target="tpu_custom_call" | custom-call | flops 9395240960 | bytes 13762560 | tf_op jit(solution)/shard_map/pallas_call | solution.py:292
  167.8 0.0 copy-start.1
  167.8 1.9 copy-done.1
  169.8 6.8 %all-gather.6.cloned.1.call-done.hidden_ref = bf16[1024,2240]{1,0:T(8,128)(2,1)} async-done(((bf16[256,2240]{1,0:T(8,128)(2,1)}), bf16[1024,2240]{1,0:T(8,128)(2,1)}) %all-gather.6.cloned.1.call-update) | async-done | bytes 4587536 | tf_op jit(solution)/shard_map/all_gather | solution.py:277
  176.6 24.8 %shard_map.95 = bf16[1024,1024]{1,0:T(8,128)(2,1)S(1)} custom-call(bf16[1024,2240]{1,0:T(8,128)(2,1)} %all-gather.6.cloned.1.call-done.hidden_ref, bf16[2240,2048]{1,0:T(8,128)(2,1)} %bitcast.27, bf16[2240,2048]{1,0:T(8,128)(2,1)} %bitcast.28, f32[9,2048]{1,0:T(8,128)S(1)} %bitcast.21, f32[9,2048]{1,0:T(8,128)S(1)} %bitcast.22, f32[3,2048]{1,0:T(4,128)S(1)} %bitcast.23, ...), custom_call_target="tpu_custom_call" | custom-call | flops 9395240960 | bytes 13762560 | tf_op jit(solution)/shard_map/pallas_call | solution.py:302
  201.3 9.0 %convolution_convert_fusion = bf16[1024,2240]{0,1:T(8,128)(2,1)} fusion(bf16[1024,1024]{1,0:T(8,128)(2,1)S(1)} %shard_map.95, bf16[1024,2240]{0,1:T(8,128)(2,1)} %param.15), kind=kOutput, calls=%fused_computation | convolution fusion | flops 4699914240 | bytes 11272192 | tf_op jit(solution)/shard_map/dot_general | solution.py:316
  210.3 6.6 %copy.19 = bf16[1024,2240]{1,0:T(8,128)(2,1)} copy(bf16[1024,2240]{0,1:T(8,128)(2,1)} %convolution_convert_fusion) | data formatting | bytes 9175040 | tf_op jit(solution)/shard_map/convert_element_type | solution.py:316
  217.0 0.0 copy-start.2
  217.0 0.0 reduce-scatter.2.cloned.1.call-update
  217.0 48.1 %reduce-scatter.2.cloned.1.call-done = bf16[256,2240]{1,0:T(8,128)(2,1)} async-done(((bf16[1024,2240]{1,0:T(8,128)(2,1)}), bf16[256,2240]{1,0:T(8,128)(2,1)}) %reduce-scatter.2.cloned.1.call-update) | async-done | bytes 1146896 | tf_op jit(solution)/shard_map/reduce_scatter | solution.py:317
  265.1 0.0 copy-done.2
  265.1 2.6 add_convert_fusion
  (3 shorter events, 0.1 us)
Async XLA Ops:
  6.5 85.8 %all-gather.4.cloned.1.call-start = ((), (), s32[]{:S(2)}) async-start(), calls=%async_computation.1 | async-start | bytes 12902400 | tf_op jit(solution)/shard_map/all_gather | solution.py:250
  7.3 136.5 %all-gather.8.cloned.1.call-start = ((), (), s32[]{:S(2)}) async-start(), calls=%async_computation.3 | async-start | bytes 5898240 | tf_op jit(solution)/shard_map/all_gather | solution.py:276
  12.2 80.1 %copy-start.5 = (bf16[8,2,16,2240]{3,2,1,0:T(8,128)(2,1)S(1)}, bf16[8,2,16,2240]{3,2,1,0:T(8,128)(2,1)}, u32[]{:S(2)}) copy-start(bf16[8,2,16,2240]{3,2,1,0:T(8,128)(2,1)} %param.9) | copy-start | bytes 3440644
  100.6 75.9 %all-gather.6.cloned.1.call-start = ((), (), s32[]{:S(2)}) async-start(), calls=%async_computation.2 | async-start | bytes 5898240 | tf_op jit(solution)/shard_map/all_gather | solution.py:277
  102.4 28.3 %collective-permute-start = (bf16[256,2240]{0,1:T(8,128)(2,1)S(1)}, bf16[256,2240]{0,1:T(8,128)(2,1)S(1)}, u32[]{:S(2)}, u32[]{:S(2)}) collective-permute-start(bf16[256,2240]{0,1:T(8,128)(2,1)S(1)} %copy.17), channel_id=1, source_target_pairs={{0,4},{4,8},{8,12},{12,16},{16,20},{20,24},{24,28},{1,5},{5,9},{9,... | collective-permute-start | bytes 3440648 | tf_op jit(solution)/shard_map/ppermute | solution.py:27
  132.2 132.9 %reduce-scatter.2.cloned.1.call-start = ((), (), s32[]{:S(2)}) async-start(), calls=%async_computation.4 | async-start | bytes 5898240 | tf_op jit(solution)/shard_map/reduce_scatter | solution.py:317
  132.4 11.1 %copy-start.3 = (f32[3,3,2,1024]{3,2,1,0:T(2,128)S(1)}, f32[3,3,2,1024]{3,2,1,0:T(2,128)}, u32[]{:S(2)}) copy-start(f32[3,3,2,1024]{3,2,1,0:T(2,128)} %param.16) | copy-start | bytes 221188
  132.5 11.2 %copy-start.4 = (f32[3,2,1024]{2,1,0:T(2,128)S(1)}, f32[3,2,1024]{2,1,0:T(2,128)}, u32[]{:S(2)}) copy-start(f32[3,2,1024]{2,1,0:T(2,128)} %param.17) | copy-start | bytes 73732
  143.7 2.7 copy-start
  167.8 2.0 copy-start.1
  217.0 48.2 %copy-start.2 = (bf16[256,2240]{1,0:T(8,128)(2,1)S(1)}, bf16[256,2240]{1,0:T(8,128)(2,1)}, u32[]{:S(2)}) copy-start(bf16[256,2240]{1,0:T(8,128)(2,1)} %fusion) | copy-start | bytes 3440644
Sparse Core Ops, SparseCore 0:
  8.9 83.4 all-gather.3
  100.7 36.7 all-gather.7
  139.1 37.4 all-gather.5
  217.1 47.9 reduce-scatter.1

commit v2 on v1

--- a/solution.py
+++ b/solution.py
@@ -233,6 +233,82 @@
         return carry
 
     lax.fori_loop(0, hidden_ref.shape[0] // stride, body, 0)
+
+
+def scatter_sum_kernel(
+    rows, chunks, product_ref, hidden_ref, out_ref, got, sums, landed, send1, recv1, send2, recv2
+):
+    blk = lax.axis_index("blk")
+    tile = lax.axis_index("tile")
+    core = tile % 2
+    y = tile // 2
+    order = [step % rows for step in range(1, rows + 1)]
+
+    barrier = pltpu.get_barrier_semaphore()
+    pl.semaphore_signal(barrier, inc=1, device_id=(blk, y * 2 + 1 - core), device_id_type=MESH)
+    for step in range(1, rows):
+        pl.semaphore_signal(
+            barrier, inc=1, device_id=(blk, ((y + step) % rows) * 2 + core), device_id_type=MESH
+        )
+    pl.semaphore_wait(barrier, rows)
+
+    first = {}
+    for step in order:
+        there = (y + step) % rows
+        for k in range(chunks):
+            slot = step * chunks + k
+            copy = pltpu.make_async_remote_copy(
+                src_ref=product_ref.at[there * 2 + 1 - core, k], dst_ref=got.at[step, k],
+                send_sem=send1.at[slot], recv_sem=recv1.at[slot],
+                device_id=(blk, y * 2 + 1 - core), device_id_type=MESH,
+            )
+            copy.start()
+            first[step, k] = copy
+    second = {}
+    for k in range(chunks):
+        for step in range(1, rows):
+            there = (y + step) % rows
+            slot = step * chunks + k
+            first[step, k].wait_recv()
+            chip = product_ref[there * 2 + core, k].astype(jnp.float32) + got[step, k].astype(
+                jnp.float32
+            )
+            sums[step, k] = chip.astype(jnp.bfloat16)
+            copy = pltpu.make_async_remote_copy(
+                src_ref=sums.at[step, k], dst_ref=landed.at[step, k],
+                send_sem=send2.at[slot], recv_sem=recv2.at[slot],
+                device_id=(blk, there * 2 + core), device_id_type=MESH,
+            )
+            copy.start()
+            second[step, k] = copy
+    for k in range(chunks):
+        first[0, k].wait_recv()
+        total = product_ref[tile, k].astype(jnp.float32) + got[0, k].astype(jnp.float32)
+        for step in range(1, rows):
+            second[step, k].wait_recv()
+            total = total + landed[step, k].astype(jnp.float32)
+        out_ref[k] = (hidden_ref[k].astype(jnp.float32) + total).astype(jnp.bfloat16)
+    for copy in list(first.values()) + list(second.values()):
+        copy.wait_send()
+
+
+def scatter_sum(product, hidden, tiles):
+    rows = tiles // 2
+    chunks = 4
+    tokens, width = hidden.shape
+    piece = (chunks, tokens // chunks, width)
+    bf16 = jnp.bfloat16
+    sems = [pltpu.SemaphoreType.DMA((rows * chunks,))] * 4
+    return pl.pallas_call(
+        functools.partial(scatter_sum_kernel, rows, chunks),
+        out_shape=jax.ShapeDtypeStruct(piece, bf16),
+        in_specs=vmem_specs(2),
+        out_specs=vmem_specs(1)[0],
+        scratch_shapes=[pltpu.VMEM((rows,) + piece, bf16)] * 3 + sems,
+        compiler_params=pltpu.CompilerParams(
+            collective_id=1, has_side_effects=True, vmem_limit_bytes=40 * 2**20
+        ),
+    )(product.reshape((tiles,) + piece), hidden.reshape(piece))
 
 
 def on_device(
@@ -314,8 +390,7 @@
     )(before_all, w_flat, w_flat, space, space, time, time, spatial, spatial)
 
     product = jnp.dot(gated_out, w_down, preferred_element_type=jnp.float32).astype(bf16)
-    ffn_out = lax.psum_scatter(product, "tile", scatter_dimension=0, tiled=True)
-    layer_out = (hidden.astype(jnp.float32) + ffn_out.astype(jnp.float32)).astype(bf16)
+    layer_out = scatter_sum(product, hidden, tiles)
     return layer_out.reshape(queries.shape)
 
 

time: 275 us -> 258 us (0.938)
  waiting for transfers between devices: 125 us -> 77.2 us
  Pallas kernels: 86.4 us -> 117 us
  local copies, waits for them, and re-layouts: 25.7 us -> 29.1 us
    reduce_scatter x1 -> x0, waiting for transfers between devices: 48.1 us -> none  [on_device(): ffn_out = lax.psum_scatter(product, 'tile', scatter_dimension=0, tiled=True)]
    pallas_call x0 -> x1, Pallas kernels: none -> 30.2 us  [scatter_sum(): pl.pallas_call(functools.partial(scatter_sum_kernel, rows, chunks), out_s...]
    unnamed x16 -> x19, local copies, waits for them, and re-layouts: 15.9 us -> 19.2 us
  transfers between devices with their start and end apart: 5 -> 4, of which waited for: 4 -> 3; matrix products, arithmetic and copies ran while one was open for 5% -> 6% of each run, Pallas kernels for 22% -> 24%
where the time goes in v2:
time: 258 us; the launch traced here: 257 us
  Pallas kernels  117 us (45%)
  waiting for transfers between devices  77.2 us (30%)
  local copies, waits for them, and re-layouts  29.1 us (11%)
  matrix products  17.3 us (7%)
  between operations  13.2 us (5%)
  starting transfers between devices  3.7 us (1%)
    all_gather x1, waiting for transfers between devices, on_device(): w_full = lax.all_gather(w_output, 'tile', axis=0, tiled=True)  44.7 us
    pallas_call x1, Pallas kernels, scatter_sum(): pl.pallas_call(functools.partial(scatter_sum_kernel, rows, chunks), out_s...  30.2 us
    pallas_call x1, Pallas kernels, exchange_states(): pl.pallas_call(functools.partial(exchange_kernel, blocks, pair, tiles), o...  28.3 us
    pallas_call x1, Pallas kernels, on_device(): pl.pallas_call(functools.partial(gated_kernel, stride, col_count, chunk),...  24.8 us
    ppermute x1, waiting for transfers between devices, shifted(): return lax.ppermute(x, axis, pairs)  24.7 us
    pallas_call x1, Pallas kernels, on_device(): pl.pallas_call(functools.partial(spatial_kernel, stride, col_count, chunk...  21.4 us
    unnamed x19, local copies, waits for them, and re-layouts  19.2 us
    dot_general x1, matrix products, on_device(): jnp.dot(gated_out, w_down, preferred_element_type=jnp.float32).astype(bf16)  9.01 us
  transfers between devices with their start and end apart: 4, of which 3 were waited for; matrix products, arithmetic and copies ran while one was open for 6% of the time, Pallas kernels for 24%

profile of v2, /device:TPU:0, one launch (start us, length us, event | category | flops | bytes accessed | tf_op | source)
XLA Modules:
  0.0 257.2 jit_solution(5044096646404809554)
XLA Ops:
  6.5 0.0 all-gather.4.cloned.1.call-start
  6.5 0.7 all-gather.4.cloned.1.call-update
  7.3 0.0 all-gather.8.cloned.1.call-start
  7.3 4.9 %shard_map.91 = bf16[24,112,128]{2,1,0:T(8,128)(2,1)} custom-call(bf16[256,2240]{1,0:T(8,128)(2,1)} %bitcast.36, bf16[256,2240]{1,0:T(8,128)(2,1)} %bitcast.37), custom_call_target="tpu_custom_call" | custom-call | tf_op jit(solution)/shard_map/pallas_call | solution.py:328
  12.2 0.0 copy-start.6
  12.2 28.3 %shard_map.92 = bf16[8,3,112,128]{3,2,1,0:T(8,128)(2,1)} custom-call(bf16[8,3,112,128]{3,2,1,0:T(8,128)(2,1)} %bitcast.35), custom_call_target="tpu_custom_call" | custom-call | tf_op jit(solution)/shard_map/pallas_call | solution.py:137
  40.5 7.1 %shard_map.93 = bf16[256,2240]{1,0:T(8,128)(2,1)} custom-call(bf16[256,2240]{1,0:T(8,128)(2,1)} %bitcast.38, bf16[24,112,128]{2,1,0:T(8,128)(2,1)} %bitcast.34), custom_call_target="tpu_custom_call" | custom-call | tf_op jit(solution)/shard_map/pallas_call | solution.py:337
  47.6 44.7 %all-gather.4.cloned.1.call-done = bf16[2240,2240]{1,0:T(8,128)(2,1)} async-done(((bf16[560,2240]{1,0:T(8,128)(2,1)}), bf16[2240,2240]{1,0:T(8,128)(2,1)}) %all-gather.4.cloned.1.call-update) | async-done | bytes 10035216 | tf_op jit(solution)/shard_map/all_gather | solution.py:326
  92.3 0.0 copy-done.6
  92.3 8.3 %fusion = bf16[256,2240]{1,0:T(8,128)(2,1)} fusion(bf16[256,2240]{1,0:T(8,128)(2,1)} %shard_map.93, bf16[2240,2240]{1,0:T(8,128)(2,1)} %all-gather.4.cloned.1.call-done, bf16[256,2240]{1,0:T(8,128)(2,1)S(1)} %bitcast.42), kind=kOutput, calls=%fused_computation.2 | convolution fusion | flops 2570731520 | bytes 13475840 | tf_op jit(solution)/shard_map/dot_general | solution.py:344
  100.6 0.0 all-gather.8.cloned.1.call-update
  100.6 0.0 all-gather.6.cloned.1.call-start
  100.7 1.7 copy.13
  102.4 3.6 %collective-permute-start = (bf16[256,2240]{0,1:T(8,128)(2,1)S(1)}, bf16[256,2240]{0,1:T(8,128)(2,1)S(1)}, u32[]{:S(2)}, u32[]{:S(2)}) collective-permute-start(bf16[256,2240]{0,1:T(8,128)(2,1)S(1)} %copy.13), channel_id=1, source_target_pairs={{0,4},{4,8},{8,12},{12,16},{16,20},{20,24},{24,28},{1,5},{5,9},{9,... | collective-permute-start | bytes 3440648 | tf_op jit(solution)/shard_map/ppermute | solution.py:27
  106.0 24.7 %collective-permute-done = bf16[256,2240]{0,1:T(8,128)(2,1)S(1)} collective-permute-done((bf16[256,2240]{0,1:T(8,128)(2,1)S(1)}, bf16[256,2240]{0,1:T(8,128)(2,1)S(1)}, u32[]{:S(2)}, u32[]{:S(2)}) %collective-permute-start) | collective-permute-done | bytes 1146912 | tf_op jit(solution)/shard_map/ppermute | solution.py:27
  130.7 1.5 copy.14
  132.2 0.0 all-gather.6.cloned.1.call-update
  132.2 0.0 copy-start.4
  132.2 0.0 copy-start.5
  132.2 11.1 %copy.17 = bf16[280,8,2,1024]{3,1,2,0:T(8,128)(2,1)} copy(bf16[280,8,2,1024]{3,2,1,0:T(2,128)(2,1)} %bitcast.30) | data formatting | bytes 18350080
  143.3 0.0 copy-done.4
  143.4 0.0 copy-done.5
  143.5 0.0 all-gather.8.cloned.1.call-done.hidden_ref
  143.5 0.0 copy-start.2
  143.5 2.6 %copy-done.2 = bf16[1024,2240]{1,0:T(8,128)(2,1)S(1)} copy-done((bf16[1024,2240]{1,0:T(8,128)(2,1)S(1)}, bf16[1024,2240]{1,0:T(8,128)(2,1)}, u32[]{:S(2)}) %copy-start.2) | copy-done | bytes 4587544
  146.1 21.4 %shard_map.94.ov_ref.og_ref = bf16[1024,2048]{1,0:T(8,128)(2,1)S(1)} custom-call(bf16[1024,2240]{1,0:T(8,128)(2,1)S(1)} %copy-done.2, bf16[2240,2048]{1,0:T(8,128)(2,1)} %bitcast.31, f32[9,2048]{1,0:T(8,128)S(1)} %bitcast.25), custom_call_target="tpu_custom_call" | custom-call | flops 9395240960 | bytes 13762560 | tf_op jit(solution)/shard_map/pallas_call | solution.py:368
  167.5 0.0 copy-start.3
  167.5 1.9 copy-done.3
  169.5 7.1 %all-gather.6.cloned.1.call-done.hidden_ref = bf16[1024,2240]{1,0:T(8,128)(2,1)} async-done(((bf16[256,2240]{1,0:T(8,128)(2,1)}), bf16[1024,2240]{1,0:T(8,128)(2,1)}) %all-gather.6.cloned.1.call-update) | async-done | bytes 4587536 | tf_op jit(solution)/shard_map/all_gather | solution.py:353
  176.6 24.8 %shard_map.95 = bf16[1024,1024]{1,0:T(8,128)(2,1)S(1)} custom-call(bf16[1024,2240]{1,0:T(8,128)(2,1)} %all-gather.6.cloned.1.call-done.hidden_ref, bf16[2240,2048]{1,0:T(8,128)(2,1)} %bitcast.32, bf16[2240,2048]{1,0:T(8,128)(2,1)} %bitcast.33, f32[9,2048]{1,0:T(8,128)S(1)} %bitcast.26, f32[9,2048]{1,0:T(8,128)S(1)} %bitcast.27, f32[3,2048]{1,0:T(4,128)S(1)} %bitcast.28, ...), custom_call_target="tpu_custom_call" | custom-call | flops 9395240960 | bytes 13762560 | tf_op jit(solution)/shard_map/pallas_call | solution.py:378
  201.3 9.0 %convolution_convert_fusion = bf16[1024,2240]{0,1:T(8,128)(2,1)} fusion(bf16[1024,1024]{1,0:T(8,128)(2,1)S(1)} %shard_map.95, bf16[1024,2240]{0,1:T(8,128)(2,1)} %param.15), kind=kOutput, calls=%fused_computation | convolution fusion | flops 4699914240 | bytes 11272192 | tf_op jit(solution)/shard_map/dot_general | solution.py:392
  210.3 0.0 copy-start.1
  210.4 6.7 %copy.15 = bf16[1024,2240]{1,0:T(8,128)(2,1)} copy(bf16[1024,2240]{0,1:T(8,128)(2,1)} %convolution_convert_fusion) | data formatting | bytes 9175040 | tf_op jit(solution)/shard_map/convert_element_type | solution.py:392
  217.1 0.0 copy-done.1
  217.1 0.0 copy-start
  217.1 2.3 copy-done
  219.4 30.2 %shard_map.96 = bf16[4,64,2240]{2,1,0:T(8,128)(2,1)S(1)} custom-call(bf16[4,4,64,2240]{3,2,1,0:T(8,128)(2,1)S(1)} %bitcast.22, bf16[4,64,2240]{2,1,0:T(8,128)(2,1)S(1)} %bitcast.23), custom_call_target="tpu_custom_call" | custom-call | tf_op jit(solution)/shard_map/pallas_call | solution.py:302
  249.6 1.0 copy.21
  (3 shorter events, 0.1 us)
Async XLA Ops:
  6.5 85.8 %all-gather.4.cloned.1.call-start = ((), (), s32[]{:S(2)}) async-start(), calls=%async_computation | async-start | bytes 12902400 | tf_op jit(solution)/shard_map/all_gather | solution.py:326
  7.3 136.2 %all-gather.8.cloned.1.call-start = ((), (), s32[]{:S(2)}) async-start(), calls=%async_computation.2 | async-start | bytes 5898240 | tf_op jit(solution)/shard_map/all_gather | solution.py:352
  12.2 80.1 %copy-start.6 = (bf16[8,2,16,2240]{3,2,1,0:T(8,128)(2,1)S(1)}, bf16[8,2,16,2240]{3,2,1,0:T(8,128)(2,1)}, u32[]{:S(2)}) copy-start(bf16[8,2,16,2240]{3,2,1,0:T(8,128)(2,1)} %param.9) | copy-start | bytes 3440644
  100.6 75.9 %all-gather.6.cloned.1.call-start = ((), (), s32[]{:S(2)}) async-start(), calls=%async_computation.1 | async-start | bytes 5898240 | tf_op jit(solution)/shard_map/all_gather | solution.py:353
  102.4 28.3 %collective-permute-start = (bf16[256,2240]{0,1:T(8,128)(2,1)S(1)}, bf16[256,2240]{0,1:T(8,128)(2,1)S(1)}, u32[]{:S(2)}, u32[]{:S(2)}) collective-permute-start(bf16[256,2240]{0,1:T(8,128)(2,1)S(1)} %copy.13), channel_id=1, source_target_pairs={{0,4},{4,8},{8,12},{12,16},{16,20},{20,24},{24,28},{1,5},{5,9},{9,... | collective-permute-start | bytes 3440648 | tf_op jit(solution)/shard_map/ppermute | solution.py:27
  132.2 11.1 %copy-start.4 = (f32[3,3,2,1024]{3,2,1,0:T(2,128)S(1)}, f32[3,3,2,1024]{3,2,1,0:T(2,128)}, u32[]{:S(2)}) copy-start(f32[3,3,2,1024]{3,2,1,0:T(2,128)} %param.16) | copy-start | bytes 221188
  132.2 11.2 %copy-start.5 = (f32[3,2,1024]{2,1,0:T(2,128)S(1)}, f32[3,2,1024]{2,1,0:T(2,128)}, u32[]{:S(2)}) copy-start(f32[3,2,1024]{2,1,0:T(2,128)} %param.17) | copy-start | bytes 73732
  143.5 2.6 %copy-start.2 = (bf16[1024,2240]{1,0:T(8,128)(2,1)S(1)}, bf16[1024,2240]{1,0:T(8,128)(2,1)}, u32[]{:S(2)}) copy-start(bf16[1024,2240]{1,0:T(8,128)(2,1)} %all-gather.8.cloned.1.call-done.hidden_ref) | copy-start | bytes 13762564
  167.5 2.0 copy-start.3
  210.3 6.7 %copy-start.1 = (bf16[256,2240]{1,0:T(8,128)(2,1)S(1)}, bf16[256,2240]{1,0:T(8,128)(2,1)}, u32[]{:S(2)}) copy-start(bf16[256,2240]{1,0:T(8,128)(2,1)} %fusion) | copy-start | bytes 3440644
  217.1 2.3 copy-start
Sparse Core Ops, SparseCore 0:
  8.9 83.4 all-gather.3
  100.7 36.7 all-gather.7
  139.1 37.4 all-gather.5

commit v3 on v2

--- a/solution.py
+++ b/solution.py
@@ -46,8 +46,8 @@
 
 
 def exchange_kernel(
-    blocks, pair, tiles, kv_ref, state_ref, got1, got2, total, block_send, final_send, states,
-    send1, recv1, send2, recv2, send3, recv3,
+    blocks, pair, tiles, kv_ref, w_ref, state_ref, w_out, got1, got2, total, block_send, final_send,
+    states, send1, recv1, send2, recv2, send3, recv3, send_w, recv_w, send_relay, recv_relay, own_w,
 ):
     group = pair * tiles
     blk = lax.axis_index("blk")
@@ -79,6 +79,25 @@
         )
         copy.start()
         first.append(copy)
+
+    rows = tiles // 2
+    core = tile % 2
+    y = tile // 2
+    chunks = w_ref.shape[0]
+    partner = y * 2 + 1 - core
+    own = pltpu.make_async_copy(w_ref, w_out.at[tile], own_w)
+    own.start()
+    direct = {}
+    for k in range(chunks):
+        for step in range(rows):
+            target = partner if step == 0 else ((y + step) % rows) * 2 + core
+            direct[step, k] = pltpu.make_async_remote_copy(
+                src_ref=w_ref.at[k], dst_ref=w_out.at[tile, k],
+                send_sem=send_w.at[step * chunks + k], recv_sem=recv_w.at[step * chunks + k],
+                device_id=(blk, target), device_id_type=MESH,
+            )
+            direct[step, k].start()
+
     total[...] = kv_ref[rank].astype(jnp.float32)
     for step in range(1, group):
         first[step - 1].wait_recv()
@@ -129,16 +148,41 @@
         def _():
             later(step).wait_send()
 
-
-def exchange_states(kv, blocks, pair, tiles):
+    relays = []
+    for k in range(chunks):
+        for step in range(1, rows):
+            source = ((y + rows - step) % rows) * 2 + core
+            direct[step, k].wait_recv()
+            relay = pltpu.make_async_remote_copy(
+                src_ref=w_out.at[source, k], dst_ref=w_out.at[source, k],
+                send_sem=send_relay.at[step * chunks + k],
+                recv_sem=recv_relay.at[step * chunks + k],
+                device_id=(blk, partner), device_id_type=MESH,
+            )
+            relay.start()
+            relays.append(relay)
+    for k in range(chunks):
+        direct[0, k].wait_recv()
+    for relay in relays:
+        relay.wait_recv()
+    for copy in list(direct.values()) + relays:
+        copy.wait_send()
+    own.wait()
+
+
+def exchange_states(kv, w, blocks, pair, tiles):
     group = pair * tiles
     piece = kv.shape[1:]
     dma = pltpu.SemaphoreType.DMA
+    copies = (tiles // 2) * w.shape[0]
     return pl.pallas_call(
         functools.partial(exchange_kernel, blocks, pair, tiles),
-        out_shape=jax.ShapeDtypeStruct(kv.shape, jnp.bfloat16),
-        in_specs=vmem_specs(1),
-        out_specs=vmem_specs(1)[0],
+        out_shape=(
+            jax.ShapeDtypeStruct(kv.shape, jnp.bfloat16),
+            jax.ShapeDtypeStruct((tiles,) + w.shape, jnp.bfloat16),
+        ),
+        in_specs=vmem_specs(2),
+        out_specs=(vmem_specs(1)[0], pl.BlockSpec(memory_space=pl.ANY)),
         scratch_shapes=[
             pltpu.VMEM((group,) + piece, jnp.bfloat16),
             pltpu.VMEM((blocks,) + piece, jnp.bfloat16),
@@ -152,9 +196,11 @@
             dma((blocks,)),
             dma((group,)),
             dma((group,)),
-        ],
+        ]
+        + [dma((copies,))] * 4
+        + [dma],
         compiler_params=pltpu.CompilerParams(collective_id=0, has_side_effects=True),
-    )(kv)
+    )(kv, w)
 
 
 def attention_kernel(query_ref, state_ref, out_ref):
@@ -323,17 +369,18 @@
     per_rank = -(-HEADS // group)
     bf16 = jnp.bfloat16
 
-    w_full = lax.all_gather(w_output, "tile", axis=0, tiled=True)
-
     kv = pl.pallas_call(
         local_state_kernel,
         out_shape=jax.ShapeDtypeStruct((group * per_rank, HEAD_DIM, LANES), bf16),
         in_specs=vmem_specs(2),
         out_specs=vmem_specs(1)[0],
     )(key_rows.reshape(tokens, width), value_rows.reshape(tokens, width))
-    state = exchange_states(
-        kv.reshape(group, per_rank, HEAD_DIM, LANES), blocks, pair, tiles
-    ).reshape(group * per_rank, HEAD_DIM, LANES)
+    state, w_full = exchange_states(
+        kv.reshape(group, per_rank, HEAD_DIM, LANES), w_output.reshape(5, -1, width), blocks, pair,
+        tiles,
+    )
+    state = state.reshape(group * per_rank, HEAD_DIM, LANES)
+    w_full = w_full.reshape(width, width)
     attended = pl.pallas_call(
         attention_kernel,
         out_shape=jax.ShapeDtypeStruct((tokens, width), bf16),

time: 258 us -> 269 us (1.043)
  Pallas kernels: 117 us -> 174 us
  waiting for transfers between devices: 77.2 us -> 31.1 us
    pallas_call x1, Pallas kernels: 28.3 us -> 85.2 us  [exchange_states(): pl.pallas_call(functools.partial(exchange_kernel, blocks, pair, tiles), o...]
    all_gather x1 -> x0, waiting for transfers between devices: 44.7 us -> none  [on_device(): w_full = lax.all_gather(w_output, 'tile', axis=0, tiled=True)]
  transfers between devices with their start and end apart: 4 -> 3, of which waited for: 3 -> 2; matrix products, arithmetic and copies ran while one was open for 6% -> 5% of each run, Pallas kernels for 24% -> 8%
where the time goes in v3:
time: 269 us; the launch traced here: 268 us
  Pallas kernels  174 us (65%)
  waiting for transfers between devices  31.1 us (12%)
  local copies, waits for them, and re-layouts  29.2 us (11%)
  matrix products  17.3 us (6%)
  between operations  13.5 us (5%)
  starting transfers between devices  3.66 us (1%)
    pallas_call x1, Pallas kernels, exchange_states(): pl.pallas_call(functools.partial(exchange_kernel, blocks, pair, tiles), o...  85.2 us
    pallas_call x1, Pallas kernels, scatter_sum(): pl.pallas_call(functools.partial(scatter_sum_kernel, rows, chunks), out_s...  30.2 us
    pallas_call x1, Pallas kernels, on_device(): pl.pallas_call(functools.partial(gated_kernel, stride, col_count, chunk),...  24.8 us
    ppermute x1, waiting for transfers between devices, shifted(): return lax.ppermute(x, axis, pairs)  24.5 us
    pallas_call x1, Pallas kernels, on_device(): pl.pallas_call(functools.partial(spatial_kernel, stride, col_count, chunk...  21.4 us
    unnamed x19, local copies, waits for them, and re-layouts  19.3 us
    dot_general x1, matrix products, on_device(): jnp.dot(gated_out, w_down, preferred_element_type=jnp.float32).astype(bf16)  9.01 us
    dot_general x1, matrix products, on_device(): attn_out = jnp.dot(attended, w_full, preferred_element_type=jnp.float32)  8.26 us
  transfers between devices with their start and end apart: 3, of which 2 were waited for; matrix products, arithmetic and copies ran while one was open for 5% of the time, Pallas kernels for 8%

profile of v3, /device:TPU:0, one launch (start us, length us, event | category | flops | bytes accessed | tf_op | source)
XLA Modules:
  0.0 268.3 jit_solution(10720335380878356429)
XLA Ops:
  6.5 0.0 all-gather.5.cloned.1.call-start
  6.5 4.9 %shard_map.91 = bf16[24,112,128]{2,1,0:T(8,128)(2,1)} custom-call(bf16[256,2240]{1,0:T(8,128)(2,1)} %bitcast.38, bf16[256,2240]{1,0:T(8,128)(2,1)} %bitcast.39), custom_call_target="tpu_custom_call" | custom-call | tf_op jit(solution)/shard_map/pallas_call | solution.py:372
  11.5 0.0 copy-start.6
  11.5 85.2 %shard_map.92 = (bf16[8,3,112,128]{3,2,1,0:T(8,128)(2,1)}, bf16[4,5,112,2240]{3,2,1,0:T(8,128)(2,1)}) custom-call(bf16[8,3,112,128]{3,2,1,0:T(8,128)(2,1)} %bitcast.36, bf16[5,112,2240]{2,1,0:T(8,128)(2,1)} %bitcast.37), custom_call_target="tpu_custom_call" | custom-call | tf_op jit(solution)/shard_map/pallas_call | solution.py:178
  96.7 7.1 %shard_map.93 = bf16[256,2240]{1,0:T(8,128)(2,1)} custom-call(bf16[256,2240]{1,0:T(8,128)(2,1)} %bitcast.40, bf16[24,112,128]{2,1,0:T(8,128)(2,1)} %bitcast.41), custom_call_target="tpu_custom_call" | custom-call | tf_op jit(solution)/shard_map/pallas_call | solution.py:384
  103.8 0.0 copy-done.6
  103.8 8.3 %fusion = bf16[256,2240]{1,0:T(8,128)(2,1)} fusion(bf16[256,2240]{1,0:T(8,128)(2,1)} %shard_map.93, bf16[2240,2240]{1,0:T(8,128)(2,1)} %bitcast.45, bf16[256,2240]{1,0:T(8,128)(2,1)S(1)} %bitcast.46), kind=kOutput, calls=%fused_computation.2 | convolution fusion | flops 2570731520 | bytes 13475840 | tf_op jit(solution)/shard_map/dot_general | solution.py:391
  112.1 0.0 all-gather.5.cloned.1.call-update
  112.1 0.0 all-gather.3.cloned.1.call-start
  112.1 1.7 copy.13
  113.8 3.6 %collective-permute-start = (bf16[256,2240]{0,1:T(8,128)(2,1)S(1)}, bf16[256,2240]{0,1:T(8,128)(2,1)S(1)}, u32[]{:S(2)}, u32[]{:S(2)}) collective-permute-start(bf16[256,2240]{0,1:T(8,128)(2,1)S(1)} %copy.13), channel_id=1, source_target_pairs={{0,4},{4,8},{8,12},{12,16},{16,20},{20,24},{24,28},{1,5},{5,9},{9,... | collective-permute-start | bytes 3440648 | tf_op jit(solution)/shard_map/ppermute | solution.py:27
  117.5 24.5 %collective-permute-done = bf16[256,2240]{0,1:T(8,128)(2,1)S(1)} collective-permute-done((bf16[256,2240]{0,1:T(8,128)(2,1)S(1)}, bf16[256,2240]{0,1:T(8,128)(2,1)S(1)}, u32[]{:S(2)}, u32[]{:S(2)}) %collective-permute-start) | collective-permute-done | bytes 1146912 | tf_op jit(solution)/shard_map/ppermute | solution.py:27
  142.0 1.5 copy.14
  143.5 0.0 all-gather.3.cloned.1.call-update
  143.5 0.0 copy-start.4
  143.5 0.0 copy-start.5
  143.6 11.1 %copy.17 = bf16[280,8,2,1024]{3,1,2,0:T(8,128)(2,1)} copy(bf16[280,8,2,1024]{3,2,1,0:T(2,128)(2,1)} %bitcast.32) | data formatting | bytes 18350080
  154.7 0.0 copy-done.4
  154.8 0.0 copy-done.5
  154.8 0.0 all-gather.5.cloned.1.call-done.hidden_ref
  154.8 0.0 copy-start.2
  154.8 2.8 %copy-done.2 = bf16[1024,2240]{1,0:T(8,128)(2,1)S(1)} copy-done((bf16[1024,2240]{1,0:T(8,128)(2,1)S(1)}, bf16[1024,2240]{1,0:T(8,128)(2,1)}, u32[]{:S(2)}) %copy-start.2) | copy-done | bytes 4587544
  157.6 21.4 %shard_map.94.ov_ref.og_ref = bf16[1024,2048]{1,0:T(8,128)(2,1)S(1)} custom-call(bf16[1024,2240]{1,0:T(8,128)(2,1)S(1)} %copy-done.2, bf16[2240,2048]{1,0:T(8,128)(2,1)} %bitcast.33, f32[9,2048]{1,0:T(8,128)S(1)} %bitcast.27), custom_call_target="tpu_custom_call" | custom-call | flops 9395240960 | bytes 13762560 | tf_op jit(solution)/shard_map/pallas_call | solution.py:415
  179.0 0.0 copy-start.3
  179.0 1.9 copy-done.3
  180.9 6.5 %all-gather.3.cloned.1.call-done.hidden_ref = bf16[1024,2240]{1,0:T(8,128)(2,1)} async-done(((bf16[256,2240]{1,0:T(8,128)(2,1)}), bf16[1024,2240]{1,0:T(8,128)(2,1)}) %all-gather.3.cloned.1.call-update) | async-done | bytes 4587536 | tf_op jit(solution)/shard_map/all_gather | solution.py:400
  187.4 24.8 %shard_map.95 = bf16[1024,1024]{1,0:T(8,128)(2,1)S(1)} custom-call(bf16[1024,2240]{1,0:T(8,128)(2,1)} %all-gather.3.cloned.1.call-done.hidden_ref, bf16[2240,2048]{1,0:T(8,128)(2,1)} %bitcast.34, bf16[2240,2048]{1,0:T(8,128)(2,1)} %bitcast.35, f32[9,2048]{1,0:T(8,128)S(1)} %bitcast.28, f32[9,2048]{1,0:T(8,128)S(1)} %bitcast.29, f32[3,2048]{1,0:T(4,128)S(1)} %bitcast.30, ...), custom_call_target="tpu_custom_call" | custom-call | flops 9395240960 | bytes 13762560 | tf_op jit(solution)/shard_map/pallas_call | solution.py:425
  212.2 9.0 %convolution_convert_fusion = bf16[1024,2240]{0,1:T(8,128)(2,1)} fusion(bf16[1024,1024]{1,0:T(8,128)(2,1)S(1)} %shard_map.95, bf16[1024,2240]{0,1:T(8,128)(2,1)} %param.15), kind=kOutput, calls=%fused_computation | convolution fusion | flops 4699914240 | bytes 11272192 | tf_op jit(solution)/shard_map/dot_general | solution.py:439
  221.2 0.0 copy-start.1
  221.2 6.7 %copy.15 = bf16[1024,2240]{1,0:T(8,128)(2,1)} copy(bf16[1024,2240]{0,1:T(8,128)(2,1)} %convolution_convert_fusion) | data formatting | bytes 9175040 | tf_op jit(solution)/shard_map/convert_element_type | solution.py:439
  227.9 0.0 copy-done.1
  227.9 0.0 copy-start
  227.9 2.3 copy-done
  230.3 30.2 %shard_map.96 = bf16[4,64,2240]{2,1,0:T(8,128)(2,1)S(1)} custom-call(bf16[4,4,64,2240]{3,2,1,0:T(8,128)(2,1)S(1)} %bitcast.24, bf16[4,64,2240]{2,1,0:T(8,128)(2,1)S(1)} %bitcast.25), custom_call_target="tpu_custom_call" | custom-call | tf_op jit(solution)/shard_map/pallas_call | solution.py:348
  260.5 1.0 copy.21
  (3 shorter events, 0.1 us)
Async XLA Ops:
  6.5 148.3 %all-gather.5.cloned.1.call-start = ((), (), s32[]{:S(2)}) async-start(), calls=%async_computation.1 | async-start | bytes 5898240 | tf_op jit(solution)/shard_map/all_gather | solution.py:399
  11.5 92.3 %copy-start.6 = (bf16[8,2,16,2240]{3,2,1,0:T(8,128)(2,1)S(1)}, bf16[8,2,16,2240]{3,2,1,0:T(8,128)(2,1)}, u32[]{:S(2)}) copy-start(bf16[8,2,16,2240]{3,2,1,0:T(8,128)(2,1)} %param.9) | copy-start | bytes 3440644
  112.1 75.4 %all-gather.3.cloned.1.call-start = ((), (), s32[]{:S(2)}) async-start(), calls=%async_computation | async-start | bytes 5898240 | tf_op jit(solution)/shard_map/all_gather | solution.py:400
  113.8 28.2 %collective-permute-start = (bf16[256,2240]{0,1:T(8,128)(2,1)S(1)}, bf16[256,2240]{0,1:T(8,128)(2,1)S(1)}, u32[]{:S(2)}, u32[]{:S(2)}) collective-permute-start(bf16[256,2240]{0,1:T(8,128)(2,1)S(1)} %copy.13), channel_id=1, source_target_pairs={{0,4},{4,8},{8,12},{12,16},{16,20},{20,24},{24,28},{1,5},{5,9},{9,... | collective-permute-start | bytes 3440648 | tf_op jit(solution)/shard_map/ppermute | solution.py:27
  143.5 11.1 %copy-start.4 = (f32[3,3,2,1024]{3,2,1,0:T(2,128)S(1)}, f32[3,3,2,1024]{3,2,1,0:T(2,128)}, u32[]{:S(2)}) copy-start(f32[3,3,2,1024]{3,2,1,0:T(2,128)} %param.16) | copy-start | bytes 221188
  143.5 11.2 %copy-start.5 = (f32[3,2,1024]{2,1,0:T(2,128)S(1)}, f32[3,2,1024]{2,1,0:T(2,128)}, u32[]{:S(2)}) copy-start(f32[3,2,1024]{2,1,0:T(2,128)} %param.17) | copy-start | bytes 73732
  154.8 2.8 %copy-start.2 = (bf16[1024,2240]{1,0:T(8,128)(2,1)S(1)}, bf16[1024,2240]{1,0:T(8,128)(2,1)}, u32[]{:S(2)}) copy-start(bf16[1024,2240]{1,0:T(8,128)(2,1)} %all-gather.5.cloned.1.call-done.hidden_ref) | copy-start | bytes 13762564
  179.0 1.9 copy-start.3
  221.2 6.7 %copy-start.1 = (bf16[256,2240]{1,0:T(8,128)(2,1)S(1)}, bf16[256,2240]{1,0:T(8,128)(2,1)}, u32[]{:S(2)}) copy-start(bf16[256,2240]{1,0:T(8,128)(2,1)} %fusion) | copy-start | bytes 3440644
  227.9 2.3 copy-start
Sparse Core Ops, SparseCore 0:
  112.2 36.1 all-gather.4
  150.0 37.4 all-gather.2

commit v4 on v2

--- a/solution.py
+++ b/solution.py
@@ -311,6 +311,11 @@
     )(product.reshape((tiles,) + piece), hidden.reshape(piece))
 
 
+def project_kernel(x_ref, w_ref, out_ref):
+    product = jnp.dot(x_ref[...], w_ref[...], preferred_element_type=jnp.float32)
+    out_ref[...] = product.astype(jnp.bfloat16)
+
+
 def on_device(
     stream_in, queries, key_rows, value_rows, w_output, w_inner, w_down, spatial_taps, temporal_taps
 ):
@@ -389,7 +394,17 @@
         compiler_params=pltpu.CompilerParams(vmem_limit_bytes=48 * 2**20),
     )(before_all, w_flat, w_flat, space, space, time, time, spatial, spatial)
 
-    product = jnp.dot(gated_out, w_down, preferred_element_type=jnp.float32).astype(bf16)
+    product = pl.pallas_call(
+        project_kernel,
+        grid=(whole // chunk,),
+        out_shape=jax.ShapeDtypeStruct((whole, width), bf16),
+        in_specs=[
+            pl.BlockSpec((chunk, chan), lambda j: (j, 0)),
+            pl.BlockSpec((chan, width), lambda j: (0, 0)),
+        ],
+        out_specs=pl.BlockSpec((chunk, width), lambda j: (j, 0)),
+        compiler_params=pltpu.CompilerParams(vmem_limit_bytes=32 * 2**20),
+    )(gated_out, w_down)
     layer_out = scatter_sum(product, hidden, tiles)
     return layer_out.reshape(queries.shape)
 

time: 258 us -> 245 us (0.950)
  matrix products: 17.3 us -> 8.24 us
  waiting for transfers between devices: 77.2 us -> 70.6 us
  Pallas kernels: 117 us -> 122 us
    dot_general x1 -> x0, matrix products: 9.01 us -> none  [on_device(): jnp.dot(gated_out, w_down, preferred_element_type=jnp.float32).astype(bf16)]
    convert_element_type x1 -> x0, local copies, waits for them, and re-layouts: 6.73 us -> none  [on_device(): jnp.dot(gated_out, w_down, preferred_element_type=jnp.float32).astype(bf16)]
    all_gather x1, waiting for transfers between devices: 7.1 us -> 0.45 us  [on_device(): before_all = lax.all_gather(before, 'tile', axis=0, tiled=True)]
    pallas_call x0 -> x1, Pallas kernels: none -> 5.6 us  [on_device(): pl.pallas_call(project_kernel, grid=(whole // chunk,), out_shape=jax.Shap...]
    unnamed x19 -> x20, local copies, waits for them, and re-layouts: 19.2 us -> 23.7 us
  transfers between devices with their start and end apart: 4 -> 4, of which waited for: 3 -> 3; matrix products, arithmetic and copies ran while one was open for 6% -> 9% of each run, Pallas kernels for 24% -> 25%
where the time goes in v4:
time: 245 us
  Pallas kernels  122 us (50%)
  waiting for transfers between devices  70.6 us (29%)
  local copies, waits for them, and re-layouts  26.9 us (11%)
  between operations  13.2 us (5%)
  matrix products  8.24 us (3%)
  starting transfers between devices  3.7 us (2%)
    all_gather x1, waiting for transfers between devices, on_device(): w_full = lax.all_gather(w_output, 'tile', axis=0, tiled=True)  44.7 us
    pallas_call x1, Pallas kernels, scatter_sum(): pl.pallas_call(functools.partial(scatter_sum_kernel, rows, chunks), out_s...  30.2 us
    pallas_call x1, Pallas kernels, exchange_states(): pl.pallas_call(functools.partial(exchange_kernel, blocks, pair, tiles), o...  28.3 us
    pallas_call x1, Pallas kernels, on_device(): pl.pallas_call(functools.partial(gated_kernel, stride, col_count, chunk),...  24.9 us
    ppermute x1, waiting for transfers between devices, shifted(): return lax.ppermute(x, axis, pairs)  24.7 us
    unnamed x20, local copies, waits for them, and re-layouts  23.7 us
    pallas_call x1, Pallas kernels, on_device(): pl.pallas_call(functools.partial(spatial_kernel, stride, col_count, chunk...  21.2 us
    dot_general x1, matrix products, on_device(): attn_out = jnp.dot(attended, w_full, preferred_element_type=jnp.float32)  8.24 us
  transfers between devices with their start and end apart: 4, of which 3 were waited for; matrix products, arithmetic and copies ran while one was open for 9% of the time, Pallas kernels for 25%

profile of v4, /device:TPU:0, one launch (start us, length us, event | category | flops | bytes accessed | tf_op | source)
XLA Modules:
  0.0 244.9 jit_solution(8555530427074140557)
XLA Ops:
  6.5 0.0 all-gather.4.cloned.1.call-start
  6.5 0.7 all-gather.4.cloned.1.call-update
  7.3 0.0 all-gather.8.cloned.1.call-start
  7.3 4.9 %shard_map.91 = bf16[24,112,128]{2,1,0:T(8,128)(2,1)} custom-call(bf16[256,2240]{1,0:T(8,128)(2,1)} %bitcast.34, bf16[256,2240]{1,0:T(8,128)(2,1)} %bitcast.35), custom_call_target="tpu_custom_call" | custom-call | tf_op jit(solution)/shard_map/pallas_call | solution.py:333
  12.2 0.0 copy-start.6
  12.2 28.3 %shard_map.92 = bf16[8,3,112,128]{3,2,1,0:T(8,128)(2,1)} custom-call(bf16[8,3,112,128]{3,2,1,0:T(8,128)(2,1)} %bitcast.33), custom_call_target="tpu_custom_call" | custom-call | tf_op jit(solution)/shard_map/pallas_call | solution.py:137
  40.5 7.1 %shard_map.93 = bf16[256,2240]{1,0:T(8,128)(2,1)} custom-call(bf16[256,2240]{1,0:T(8,128)(2,1)} %bitcast.36, bf16[24,112,128]{2,1,0:T(8,128)(2,1)} %bitcast.32), custom_call_target="tpu_custom_call" | custom-call | tf_op jit(solution)/shard_map/pallas_call | solution.py:342
  47.6 44.7 %all-gather.4.cloned.1.call-done = bf16[2240,2240]{1,0:T(8,128)(2,1)} async-done(((bf16[560,2240]{1,0:T(8,128)(2,1)}), bf16[2240,2240]{1,0:T(8,128)(2,1)}) %all-gather.4.cloned.1.call-update) | async-done | bytes 10035216 | tf_op jit(solution)/shard_map/all_gather | solution.py:331
  92.3 0.0 copy-done.6
  92.3 8.2 %fusion = bf16[256,2240]{1,0:T(8,128)(2,1)} fusion(bf16[256,2240]{1,0:T(8,128)(2,1)} %shard_map.93, bf16[2240,2240]{1,0:T(8,128)(2,1)} %all-gather.4.cloned.1.call-done, bf16[256,2240]{1,0:T(8,128)(2,1)S(1)} %bitcast.40), kind=kOutput, calls=%fused_computation.1 | convolution fusion | flops 2570731520 | bytes 13475840 | tf_op jit(solution)/shard_map/dot_general | solution.py:349
  100.6 0.0 all-gather.8.cloned.1.call-update
  100.6 0.0 all-gather.6.cloned.1.call-start
  100.7 1.7 copy.13
  102.4 3.6 %collective-permute-start = (bf16[256,2240]{0,1:T(8,128)(2,1)S(1)}, bf16[256,2240]{0,1:T(8,128)(2,1)S(1)}, u32[]{:S(2)}, u32[]{:S(2)}) collective-permute-start(bf16[256,2240]{0,1:T(8,128)(2,1)S(1)} %copy.13), channel_id=1, source_target_pairs={{0,4},{4,8},{8,12},{12,16},{16,20},{20,24},{24,28},{1,5},{5,9},{9,... | collective-permute-start | bytes 3440648 | tf_op jit(solution)/shard_map/ppermute | solution.py:27
  106.0 24.7 %collective-permute-done = bf16[256,2240]{0,1:T(8,128)(2,1)S(1)} collective-permute-done((bf16[256,2240]{0,1:T(8,128)(2,1)S(1)}, bf16[256,2240]{0,1:T(8,128)(2,1)S(1)}, u32[]{:S(2)}, u32[]{:S(2)}) %collective-permute-start) | collective-permute-done | bytes 1146912 | tf_op jit(solution)/shard_map/ppermute | solution.py:27
  130.6 1.5 copy.14
  132.2 0.0 all-gather.6.cloned.1.call-update
  132.2 0.0 copy-start.4
  132.2 0.0 copy-start.5
  132.2 11.1 %copy.17 = bf16[280,8,2,1024]{3,1,2,0:T(8,128)(2,1)} copy(bf16[280,8,2,1024]{3,2,1,0:T(2,128)(2,1)} %bitcast.28) | data formatting | bytes 18350080
  143.3 0.0 copy-done.4
  143.4 0.0 copy-done.5
  143.5 7.1 %copy.15.w_ref = bf16[1024,2240]{1,0:T(8,128)(2,1)} copy(bf16[1024,2240]{0,1:T(8,128)(2,1)} %param.15) | data formatting | bytes 9175040 | tf_op args[6]
  150.5 0.0 all-gather.8.cloned.1.call-done.hidden_ref
  150.5 0.0 copy-start.2
  150.5 2.3 copy-done.2
  152.8 21.2 %shard_map.94.ov_ref.og_ref = bf16[1024,2048]{1,0:T(8,128)(2,1)S(1)} custom-call(bf16[1024,2240]{1,0:T(8,128)(2,1)S(1)} %copy-done.2, bf16[2240,2048]{1,0:T(8,128)(2,1)} %bitcast.29, f32[9,2048]{1,0:T(8,128)S(1)} %bitcast.23), custom_call_target="tpu_custom_call" | custom-call | flops 9395240960 | bytes 13762560 | tf_op jit(solution)/shard_map/pallas_call | solution.py:373
  174.1 0.0 copy-start.3
  174.1 2.0 copy-done.3
  176.1 0.4 all-gather.6.cloned.1.call-done.hidden_ref
  176.5 0.0 copy-start
  176.5 24.9 %shard_map.95.x_ref = bf16[1024,1024]{1,0:T(8,128)(2,1)S(1)} custom-call(bf16[1024,2240]{1,0:T(8,128)(2,1)} %all-gather.6.cloned.1.call-done.hidden_ref, bf16[2240,2048]{1,0:T(8,128)(2,1)} %bitcast.30, bf16[2240,2048]{1,0:T(8,128)(2,1)} %bitcast.31, f32[9,2048]{1,0:T(8,128)S(1)} %bitcast.24, f32[9,2048]{1,0:T(8,128)S(1)} %bitcast.25, ...), custom_call_target="tpu_custom_call" | custom-call | flops 9395240960 | bytes 13762560 | tf_op jit(solution)/shard_map/pallas_call | solution.py:383
  201.4 0.0 copy-done
  201.5 0.0 copy-start.1
  201.5 5.6 %shard_map.96 = bf16[1024,2240]{1,0:T(8,128)(2,1)S(1)} custom-call(bf16[1024,1024]{1,0:T(8,128)(2,1)S(1)} %shard_map.95.x_ref, bf16[1024,2240]{1,0:T(8,128)(2,1)S(1)} %copy-done), custom_call_target="tpu_custom_call" | custom-call | tf_op jit(solution)/shard_map/pallas_call | solution.py:397
  207.1 0.0 copy-done.1
  207.1 30.2 %shard_map.97 = bf16[4,64,2240]{2,1,0:T(8,128)(2,1)S(1)} custom-call(bf16[4,4,64,2240]{3,2,1,0:T(8,128)(2,1)S(1)} %bitcast.20, bf16[4,64,2240]{2,1,0:T(8,128)(2,1)S(1)} %bitcast.21), custom_call_target="tpu_custom_call" | custom-call | tf_op jit(solution)/shard_map/pallas_call | solution.py:302
  237.3 1.0 copy.21
  (3 shorter events, 0.1 us)
Async XLA Ops:
  6.5 85.8 %all-gather.4.cloned.1.call-start = ((), (), s32[]{:S(2)}) async-start(), calls=%async_computation | async-start | bytes 12902400 | tf_op jit(solution)/shard_map/all_gather | solution.py:331
  7.3 143.3 %all-gather.8.cloned.1.call-start = ((), (), s32[]{:S(2)}) async-start(), calls=%async_computation.2 | async-start | bytes 5898240 | tf_op jit(solution)/shard_map/all_gather | solution.py:357
  12.2 80.1 %copy-start.6 = (bf16[8,2,16,2240]{3,2,1,0:T(8,128)(2,1)S(1)}, bf16[8,2,16,2240]{3,2,1,0:T(8,128)(2,1)}, u32[]{:S(2)}) copy-start(bf16[8,2,16,2240]{3,2,1,0:T(8,128)(2,1)} %param.9) | copy-start | bytes 3440644
  100.6 75.9 %all-gather.6.cloned.1.call-start = ((), (), s32[]{:S(2)}) async-start(), calls=%async_computation.1 | async-start | bytes 5898240 | tf_op jit(solution)/shard_map/all_gather | solution.py:358
  102.4 28.3 %collective-permute-start = (bf16[256,2240]{0,1:T(8,128)(2,1)S(1)}, bf16[256,2240]{0,1:T(8,128)(2,1)S(1)}, u32[]{:S(2)}, u32[]{:S(2)}) collective-permute-start(bf16[256,2240]{0,1:T(8,128)(2,1)S(1)} %copy.13), channel_id=1, source_target_pairs={{0,4},{4,8},{8,12},{12,16},{16,20},{20,24},{24,28},{1,5},{5,9},{9,... | collective-permute-start | bytes 3440648 | tf_op jit(solution)/shard_map/ppermute | solution.py:27
  132.2 11.1 %copy-start.4 = (f32[3,3,2,1024]{3,2,1,0:T(2,128)S(1)}, f32[3,3,2,1024]{3,2,1,0:T(2,128)}, u32[]{:S(2)}) copy-start(f32[3,3,2,1024]{3,2,1,0:T(2,128)} %param.16) | copy-start | bytes 221188
  132.2 11.2 %copy-start.5 = (f32[3,2,1024]{2,1,0:T(2,128)S(1)}, f32[3,2,1024]{2,1,0:T(2,128)}, u32[]{:S(2)}) copy-start(f32[3,2,1024]{2,1,0:T(2,128)} %param.17) | copy-start | bytes 73732
  150.5 2.3 copy-start.2
  174.1 2.0 copy-start.3
  176.5 24.9 %copy-start = (bf16[1024,2240]{1,0:T(8,128)(2,1)S(1)}, bf16[1024,2240]{1,0:T(8,128)(2,1)}, u32[]{:S(2)}) copy-start(bf16[1024,2240]{1,0:T(8,128)(2,1)} %copy.15.w_ref) | copy-start | bytes 13762564
  201.5 5.6 %copy-start.1 = (bf16[256,2240]{1,0:T(8,128)(2,1)S(1)}, bf16[256,2240]{1,0:T(8,128)(2,1)}, u32[]{:S(2)}) copy-start(bf16[256,2240]{1,0:T(8,128)(2,1)} %fusion) | copy-start | bytes 3440644
Sparse Core Ops, SparseCore 0:
  8.9 83.4 all-gather.3
  100.7 36.7 all-gather.7
  139.1 37.4 all-gather.5
